TPU v7x, 32 devices: a whole 2x2x4 slice. The times are simulated.
32 devices in a mesh: ep: 8 (over z, x), rep: 4 (over y, core).
Axes of the slice: x: 2, y: 2, z: 4, core: 2. Of those that a mesh axis runs over, the one named last changes fastest.
Arguments:
- tokens: bfloat16 [4096, 4096], P(('ep', 'rep')), may hold values from -6 to 6
- expert_ids: int32 [4096, 2], P(('ep', 'rep')), may hold values from 0 to 63, as said below
- route_weights: float32 [4096, 2], P(('ep', 'rep')), may hold values from 0.1 to 1
- w_gate: bfloat16 [4, 4096, 2048], P('rep', None, 'ep'), may hold values from -0.09375 to 0.09375
- w_up: bfloat16 [4, 4096, 2048], P('rep', None, 'ep'), may hold values from -0.09375 to 0.09375
- w_down: bfloat16 [4, 2048, 4096], P('rep', 'ep'), may hold values from -0.125 to 0.125
- cotangent: bfloat16 [4096, 4096], P(('ep', 'rep')), may hold values from -6 to 6
Outputs:
- mixed: bfloat16 [4096, 4096], P(('ep', 'rep'))
- grad_tokens: bfloat16 [4096, 4096], P(('ep', 'rep'))
- grad_gate: bfloat16 [4, 4096, 2048], P('rep', None, 'ep')
- grad_up: bfloat16 [4, 4096, 2048], P('rep', None, 'ep')
- grad_down: bfloat16 [4, 2048, 4096], P('rep', 'ep')
Inputs may be any that keep to these rules, and one draw needn't show every extreme that they name: `expert_ids`: A token's two experts differ. Among the rows of one device, each expert below 4 is named at most 4 times; one of them is named exactly 4 times by every device.
All inputs are finite; a program needn't handle non-finite values.
Results may differ from a plain program's by a relative error of at most 0.0058.
Values may be sent and summed in bfloat16 or wider, within the bound.
No kernel may reach another device: no remote copies, remote signals or barrier semaphores. Data moves between devices by JAX's collectives and lax.ppermute only.
A program may use at most 128 MiB of HBM per device.

v0:
```python
import jax
import jax.numpy as jnp
from jax import lax
from jax.experimental import pallas as pl
from jax.experimental.pallas import tpu as pltpu
from jax.sharding import PartitionSpec as P


CAP = 4
BF = jnp.bfloat16
F32 = jnp.float32
VMEM = pl.BlockSpec(memory_space=pltpu.VMEM)
SMEM = pl.BlockSpec(memory_space=pltpu.SMEM)
HBM = pl.BlockSpec(memory_space=pltpu.HBM)


def call(body, out_shape, n_in, limit=12, smem=0):
    return pl.pallas_call(
        body,
        out_shape=out_shape,
        in_specs=[SMEM] * smem + [VMEM] * (n_in - smem),
        out_specs=jax.tree.map(lambda _: VMEM, out_shape),
        compiler_params=pltpu.CompilerParams(vmem_limit_bytes=limit << 20),
    )


def selection(rank_id, ids, n_rep):
    slots = n_rep * CAP
    tok = ids.shape[1]
    row = lax.broadcasted_iota(jnp.int32, (slots, tok), 0)
    expert = jnp.bitwise_xor(rank_id, row // CAP)
    first = ids[0:1, :] == expert
    second = ids[1:2, :] == expert
    member = jnp.logical_or(first, second)
    below = lax.broadcasted_iota(jnp.int32, (tok, tok), 0) < lax.broadcasted_iota(
        jnp.int32, (tok, tok), 1
    )
    earlier = jnp.dot(
        jnp.where(member, 1.0, 0.0).astype(BF),
        jnp.where(below, 1.0, 0.0).astype(BF),
        preferred_element_type=F32,
    )
    chosen = jnp.logical_and(member, earlier == (row % CAP).astype(F32))
    return chosen, first


def slot_weights(chosen, first, weights):
    both = jnp.where(first, weights[0:1, :], weights[1:2, :])
    return jnp.sum(jnp.where(chosen, both, 0.0), axis=1, keepdims=True)


def in_hbm(arrays):
    return [pltpu.with_memory_space_constraint(v, pltpu.HBM) for v in arrays]


def pack(rank_id, ids, weights, tokens, cotangent, n_rep):
    width = tokens.shape[1]
    given = [ids, weights, tokens, cotangent]

    def body(rank_ref, *refs):
        ins, outs = refs[:4], refs[4 : 4 + n_rep]
        held, sems = refs[4 + n_rep : 8 + n_rep], refs[-1]
        copies = [
            pltpu.make_async_copy(src, dst, sems.at[i])
            for i, (src, dst) in enumerate(zip(ins, held))
        ]
        for copy in copies:
            copy.start()
        copies[0].wait()
        copies[1].wait()
        chosen, first = selection(rank_ref[0], held[0][...], n_rep)
        scale = slot_weights(chosen, first, held[1][...])
        pick = jnp.where(chosen, 1.0, 0.0).astype(BF)
        copies[2].wait()
        rows = jnp.dot(pick, held[2][...], preferred_element_type=F32)
        for k in range(n_rep):
            outs[k][0:CAP, :] = rows[k * CAP : (k + 1) * CAP].astype(BF)
        copies[3].wait()
        rows = jnp.dot(pick, held[3][...], preferred_element_type=F32) * scale
        for k in range(n_rep):
            outs[k][CAP : 2 * CAP, :] = rows[k * CAP : (k + 1) * CAP].astype(BF)

    return pl.pallas_call(
        body,
        out_shape=[jax.ShapeDtypeStruct((2 * CAP, width), BF)] * n_rep,
        in_specs=[SMEM] + [HBM] * 4,
        out_specs=[VMEM] * n_rep,
        scratch_shapes=[pltpu.VMEM(v.shape, v.dtype) for v in given]
        + [pltpu.SemaphoreType.DMA((4,))],
        compiler_params=pltpu.CompilerParams(vmem_limit_bytes=12 << 20),
    )(rank_id, *in_hbm(given))


def load(*arrays):
    n = len(arrays)

    def body(*refs):
        ins, outs, turned, sems = refs[:n], refs[n : 2 * n], refs[2 * n : 3 * n], refs[3 * n]
        copies = [pltpu.make_async_copy(ins[i], outs[i], sems.at[i]) for i in range(n)]
        for copy in copies:
            copy.start()
        for i in range(n):
            copies[i].wait()
            turned[i][...] = outs[i][...].T

    out = pl.pallas_call(
        body,
        out_shape=[jax.ShapeDtypeStruct(a.shape, a.dtype) for a in arrays]
        + [jax.ShapeDtypeStruct(a.shape[::-1], a.dtype) for a in arrays],
        in_specs=[HBM] * n,
        out_specs=[VMEM] * (2 * n),
        scratch_shapes=[pltpu.SemaphoreType.DMA((n,))],
        compiler_params=pltpu.CompilerParams(vmem_limit_bytes=12 << 20),
    )(*in_hbm(arrays))
    return out[:n], out[n:]


def split(blocks):
    n = len(blocks)
    width = blocks[0].shape[1]

    def body(*refs):
        ins, (tok_ref, up_ref) = refs[:n], refs[n:]
        tok_ref[...] = jnp.concatenate([r[0:CAP, :] for r in ins], axis=0)
        up_ref[...] = jnp.concatenate([r[CAP : 2 * CAP, :] for r in ins], axis=0)

    shape = [jax.ShapeDtypeStruct((n * CAP, width), BF)] * 2
    return call(body, shape, n)(*blocks)


def streamed(compute, tiles, out_shapes, n_in, smem=0):
    n_out = len(out_shapes)

    def body(*refs):
        ins, outs = refs[:n_in], refs[n_in : n_in + n_out]
        held, sems = refs[n_in + n_out : n_in + 2 * n_out], refs[-1]
        copies = []
        state = None
        for i in range(tiles):
            state, results = compute(ins, i, state)
            for j, (where, value) in enumerate(results):
                held[j][where] = value.astype(BF)
                copy = pltpu.make_async_copy(
                    held[j].at[where], outs[j].at[where], sems.at[i * n_out + j]
                )
                copy.start()
                copies.append(copy)
        for copy in copies:
            copy.wait()

    return pl.pallas_call(
        body,
        out_shape=[jax.ShapeDtypeStruct(shape, BF) for shape in out_shapes],
        in_specs=[SMEM] * smem + [VMEM] * (n_in - smem),
        out_specs=[HBM] * n_out,
        scratch_shapes=[pltpu.VMEM(shape, BF) for shape in out_shapes]
        + [pltpu.SemaphoreType.DMA((tiles * n_out,))],
        compiler_params=pltpu.CompilerParams(vmem_limit_bytes=24 << 20),
    )


OVER_ROWS = (((0,), (0,)), ((), ()))


def unpack(rank_id, ids, weights, blocks):
    n = len(blocks)
    width = blocks[0].shape[1]
    tok = ids.shape[1]
    tiles = 4
    cols = width // tiles

    def compute(ins, i, state):
        at = slice(i * cols, (i + 1) * cols)
        if state is None:
            chosen, first = selection(ins[0][0], ins[1][...], n)
            pick = jnp.where(chosen, 1.0, 0.0).astype(BF)
            state = (pick, slot_weights(chosen, first, ins[2][...]))
        pick, scale = state
        full = jnp.concatenate([r[0:CAP, at].astype(F32) for r in ins[3:]], axis=0) * scale
        top = full.astype(BF)
        rest = full - top.astype(F32)
        middle = rest.astype(BF)
        low = (rest - middle.astype(F32)).astype(BF)
        mixed = lax.dot_general(
            jnp.concatenate([pick, pick, pick], axis=0),
            jnp.concatenate([top, middle, low], axis=0),
            OVER_ROWS,
            preferred_element_type=F32,
        )
        rows = jnp.concatenate([r[CAP : 2 * CAP, at] for r in ins[3:]], axis=0)
        grads = lax.dot_general(pick, rows, OVER_ROWS, preferred_element_type=F32)
        return state, [((slice(None), at), mixed), ((slice(None), at), grads)]

    kernel = streamed(compute, tiles, [(tok, width)] * 2, 3 + n, smem=1)
    return kernel(rank_id, ids, weights, *blocks)


def weight_grads(*jobs):
    count = len(jobs)
    shapes = [(left.shape[1], right.shape[1]) for left, right in jobs]
    flat = [v for job in jobs for v in job]
    tiles = 4

    def body(*refs):
        ins, outs = refs[: 2 * count], refs[2 * count : 3 * count]
        held, sems = refs[3 * count : 4 * count], refs[-1]
        copies = []
        for j, (m, n) in enumerate(shapes):
            left, right = ins[2 * j], ins[2 * j + 1]
            for i in range(tiles):
                if m > n:
                    at = (slice(i * m // tiles, (i + 1) * m // tiles), slice(None))
                else:
                    at = (slice(None), slice(i * n // tiles, (i + 1) * n // tiles))
                held[j][at] = lax.dot_general(
                    left[:, at[0]], right[:, at[1]], OVER_ROWS, preferred_element_type=F32
                ).astype(BF)
                copy = pltpu.make_async_copy(held[j].at[at], outs[j].at[at], sems.at[j * tiles + i])
                copy.start()
                copies.append(copy)
        for copy in copies:
            copy.wait()

    return pl.pallas_call(
        body,
        out_shape=[jax.ShapeDtypeStruct(shape, BF) for shape in shapes],
        in_specs=[VMEM] * (2 * count),
        out_specs=[HBM] * count,
        scratch_shapes=[pltpu.VMEM(shape, BF) for shape in shapes]
        + [pltpu.SemaphoreType.DMA((tiles * count,))],
        compiler_params=pltpu.CompilerParams(vmem_limit_bytes=24 << 20),
    )(*flat)


def part_types(n, rows, width, heavy):
    half = n // 2
    starts = {half, n - half + 1} if heavy > 0 else {half, half - 1}
    return [
        jax.ShapeDtypeStruct((rows, width), BF if d in starts else F32) for d in range(n)
    ]


def forward(chunks, w_gate, w_up, w_down, heavy):
    n = len(chunks)
    rows, width = chunks[0].shape
    ff = w_gate.shape[1]
    total = n * rows

    def body(*refs):
        ins, (wg, wu, wd) = refs[:n], refs[n : n + 3]
        all_ref, hidden_ref, act_ref, slope_ref = refs[n + 3 : n + 7]
        outs = refs[n + 7 :]
        for d in range(n):
            all_ref[d * rows : (d + 1) * rows, :] = ins[d][...]
        x = all_ref[...]
        pre_gate = jnp.dot(x, wg[...], preferred_element_type=F32)
        pre_up = jnp.dot(x, wu[...], preferred_element_type=F32)
        logistic = jax.nn.sigmoid(pre_gate)
        activated = pre_gate * logistic
        hidden = (activated * pre_up).astype(BF)
        hidden_ref[...] = hidden
        act_ref[...] = activated
        slope_ref[...] = pre_up * logistic * (1.0 + pre_gate * (1.0 - logistic))
        routed = jnp.dot(hidden, wd[...], preferred_element_type=F32)
        for d in range(n):
            outs[d][...] = routed[d * rows : (d + 1) * rows].astype(outs[d].dtype)

    shape = [
        jax.ShapeDtypeStruct((total, width), BF),
        jax.ShapeDtypeStruct((total, ff), BF),
        jax.ShapeDtypeStruct((total, ff), F32),
        jax.ShapeDtypeStruct((total, ff), F32),
    ] + part_types(n, rows, width, heavy)
    out = call(body, shape, n + 3, limit=24)(*chunks, w_gate, w_up, w_down)
    return out[0], out[1], out[2], out[3], out[4:]


def backward(chunks, activated, slope, gate_t, up_t, down_t, heavy):
    n = len(chunks)
    rows, width = chunks[0].shape
    ff = gate_t.shape[0]
    total = n * rows

    def body(*refs):
        ins, (act_ref, slope_ref, wgt, wut, wdt) = refs[:n], refs[n : n + 5]
        all_ref, dg_ref, du_ref = refs[n + 5 : n + 8]
        outs = refs[n + 8 :]
        for d in range(n):
            all_ref[d * rows : (d + 1) * rows, :] = ins[d][...]
        d_act = jnp.dot(all_ref[...], wdt[...], preferred_element_type=F32)
        d_up = (d_act * act_ref[...]).astype(BF)
        d_gate = (d_act * slope_ref[...]).astype(BF)
        dg_ref[...] = d_gate
        du_ref[...] = d_up
        grads = jnp.dot(d_gate, wgt[...], preferred_element_type=F32)
        grads += jnp.dot(d_up, wut[...], preferred_element_type=F32)
        for d in range(n):
            outs[d][...] = grads[d * rows : (d + 1) * rows].astype(outs[d].dtype)

    shape = [
        jax.ShapeDtypeStruct((total, width), BF),
        jax.ShapeDtypeStruct((total, ff), BF),
        jax.ShapeDtypeStruct((total, ff), BF),
    ] + part_types(n, rows, width, heavy)
    out = call(body, shape, n + 5, limit=24)(*chunks, activated, slope, gate_t, up_t, down_t)
    return out[0], out[1], out[2], out[3:]


def ring_order(n):
    return [i for i in range(0, n, 2)] + [i for i in reversed(range(1, n, 2))]


def shift(value, step):
    n, n_rep = lax.axis_size("ep"), lax.axis_size("rep")
    order = ring_order(n)
    pairs = []
    for r in range(n_rep):
        way = step
        pairs += [
            (order[i] * n_rep + r, order[(i + way) % n] * n_rep + r) for i in range(n)
        ]
    return lax.ppermute(value, ("ep", "rep"), pairs)


def ring_gather(chunk, heavy):
    n = lax.axis_size("ep")
    half = n // 2
    found = {0: chunk}
    ahead = behind = chunk
    for step in range(1, half + 1):
        ahead = shift(ahead, heavy)
        found[(-heavy * step) % n] = ahead
        if step < half:
            behind = shift(behind, -heavy)
            found[(heavy * step) % n] = behind
    return [found[d] for d in range(n)]


def ring_scatter(parts, heavy):
    n = len(parts)
    half = n // 2
    ahead = shift(parts[half], heavy)
    behind = shift(parts[(-heavy * (half - 1)) % n], -heavy)
    for step in range(1, half):
        d = (heavy * (half - step)) % n
        ahead = shift((ahead.astype(F32) + parts[d]).astype(BF), heavy)
        if step < half - 1:
            d = (-heavy * (half - 1 - step)) % n
            behind = shift((behind.astype(F32) + parts[d]).astype(BF), -heavy)
    return parts[0], ahead, behind


def finish(routed, row_grads, n):
    width = routed[0].shape[1]

    def body(*refs):
        ins, outs = refs[:6], refs[6:]
        for half in range(2):
            own, ahead, behind = ins[3 * half : 3 * half + 3]
            total = own[...] + ahead[...].astype(F32) + behind[...].astype(F32)
            for k in range(n):
                outs[k][half * CAP : (half + 1) * CAP, :] = total[k * CAP : (k + 1) * CAP].astype(BF)

    shape = [jax.ShapeDtypeStruct((2 * CAP, width), BF)] * n
    return call(body, shape, 6)(*routed, *row_grads)


def trade(blocks):
    n = lax.axis_size("rep")
    found = [blocks[0]]
    for k in range(1, n):
        found.append(lax.ppermute(blocks[k], "rep", [(i, i ^ k) for i in range(n)]))
    return found


def local(tokens, expert_ids, route_weights, w_gate, w_up, w_down, cotangent):
    n_rep = lax.axis_size("rep")
    rank_id = lax.axis_index("rep").astype(jnp.int32).reshape(1)
    ids = expert_ids.T
    weights = route_weights.T

    sent = pack(rank_id, ids, weights, tokens, cotangent, n_rep)
    token_rows, up_rows = split(trade(sent))
    plain, turned = load(w_gate[0], w_up[0], w_down[0])
    token_chunks = ring_gather(token_rows, 1)
    up_chunks = ring_gather(up_rows, -1)
    all_tokens, hidden, activated, slope, routed_parts = forward(token_chunks, *plain, 1)
    routed = ring_scatter(routed_parts, 1)
    all_ups, d_gate, d_up, grad_parts = backward(up_chunks, activated, slope, *turned, -1)
    row_grads = ring_scatter(grad_parts, -1)
    grad_gate, grad_up = weight_grads((all_tokens, d_gate), (all_tokens, d_up))
    (grad_down,) = weight_grads((hidden, all_ups))
    back = trade(finish(routed, row_grads, n_rep))
    mixed, grad_tokens = unpack(rank_id, ids, weights, back)
    return (mixed, grad_tokens, grad_gate[None], grad_up[None], grad_down[None])


def solution(mesh):
    placed = (
        P(("ep", "rep"), None),
        P(("ep", "rep"), None),
        P(("ep", "rep"), None),
        P("rep", None, "ep"),
        P("rep", None, "ep"),
        P("rep", "ep", None),
        P(("ep", "rep"), None),
    )

    return jax.shard_map(
        local,
        mesh=mesh,
        in_specs=placed,
        out_specs=(
            P(("ep", "rep"), None),
            P(("ep", "rep"), None),
            P("rep", None, "ep"),
            P("rep", None, "ep"),
            P("rep", "ep", None),
        ),
        check_vma=False,
    )
```

profile of v0, /device:TPU:0, one launch (start us, length us, event | category | flops | bytes accessed | tf_op | source)
XLA Modules:
  0.0 74.6 jit_solution(2686529192058713527)
XLA Ops:
  0.6 1.9 %shard_map.110 = (bf16[8,4096]{1,0:T(8,128)(2,1)S(1)}, bf16[8,4096]{1,0:T(8,128)(2,1)S(1)}, bf16[8,4096]{1,0:T(8,128)(2,1)S(1)}, bf16[8,4096]{1,0:T(8,128)(2,1)S(1)}) custom-call(s32[1]{0:T(128)} %bitcast.rank_ref.refs_0_, s32[2,128]{1,0:T(2,128)} %bitcast.9, f32[2,128]{1,0:T(2,128)} %bitcast.11, bf16[128,4096]{1,0:T(8,128)(2,1)} %refs_2_.1, ...), custom_call_target="tpu_custom_call" | custom-call | tf_op jit(solution)/shard_map/pallas_call | solution.py:83
  2.5 0.6 collective-permute-start
  3.1 2.6 %collective-permute-start.1 = (bf16[8,4096]{1,0:T(8,128)(2,1)S(1)}, bf16[8,4096]{1,0:T(8,128)(2,1)S(1)}, u32[]{:S(2)}, u32[]{:S(2)}) collective-permute-start(bf16[8,4096]{1,0:T(8,128)(2,1)S(1)} %get-tuple-element.50), channel_id=1, source_target_pairs={{0,2},{1,3},{2,0},{3,1},{4,6},{5,7},{6,4},{7,5},{8,10},{9,11},{10,... | collective-permute-start | bytes 196616 | tf_op jit(solution)/shard_map/ppermute | solution.py:372
  5.7 2.6 %collective-permute-done.1.refs_2_ = bf16[8,4096]{1,0:T(8,128)(2,1)S(1)} collective-permute-done((bf16[8,4096]{1,0:T(8,128)(2,1)S(1)}, bf16[8,4096]{1,0:T(8,128)(2,1)S(1)}, u32[]{:S(2)}, u32[]{:S(2)}) %collective-permute-start.1) | collective-permute-done | bytes 65568 | tf_op jit(solution)/shard_map/ppermute | solution.py:372
  8.3 1.4 %collective-permute-done.2.refs_3_ = bf16[8,4096]{1,0:T(8,128)(2,1)S(1)} collective-permute-done((bf16[8,4096]{1,0:T(8,128)(2,1)S(1)}, bf16[8,4096]{1,0:T(8,128)(2,1)S(1)}, u32[]{:S(2)}, u32[]{:S(2)}) %collective-permute-start.2) | collective-permute-done | bytes 65568 | tf_op jit(solution)/shard_map/ppermute | solution.py:372
  9.8 1.6 %collective-permute-start.6 = (bf16[16,4096]{1,0:T(8,128)(2,1)S(1)}, bf16[16,4096]{1,0:T(8,128)(2,1)S(1)}, u32[]{:S(2)}, u32[]{:S(2)}) collective-permute-start(bf16[16,4096]{1,0:T(8,128)(2,1)S(1)} %get-tuple-element.52.refs_0_), channel_id=1, source_target_pairs={{0,8},{8,16},{16,24},{24,28},{28,20},{20,12},{12,4},{4,0},{1,9},{9... | collective-permute-start | bytes 393224 | tf_op jit(solution)/shard_map/ppermute | solution.py:322
  11.4 0.4 collective-permute-start.17
  11.9 1.5 %collective-permute-start.3 = (bf16[16,4096]{1,0:T(8,128)(2,1)S(1)}, bf16[16,4096]{1,0:T(8,128)(2,1)S(1)}, u32[]{:S(2)}, u32[]{:S(2)}) collective-permute-start(bf16[16,4096]{1,0:T(8,128)(2,1)S(1)} %get-tuple-element.52.refs_0_), channel_id=1, source_target_pairs={{0,4},{8,0},{16,8},{24,16},{28,24},{20,28},{12,20},{4,12},{1,5},{9... | collective-permute-start | bytes 393224 | tf_op jit(solution)/shard_map/ppermute | solution.py:322
  13.4 2.0 %collective-permute-done.6.refs_7_ = bf16[16,4096]{1,0:T(8,128)(2,1)S(1)} collective-permute-done((bf16[16,4096]{1,0:T(8,128)(2,1)S(1)}, bf16[16,4096]{1,0:T(8,128)(2,1)S(1)}, u32[]{:S(2)}, u32[]{:S(2)}) %collective-permute-start.6) | collective-permute-done | bytes 131104 | tf_op jit(solution)/shard_map/ppermute | solution.py:322
  15.4 1.6 %collective-permute-start.7 = (bf16[16,4096]{1,0:T(8,128)(2,1)S(1)}, bf16[16,4096]{1,0:T(8,128)(2,1)S(1)}, u32[]{:S(2)}, u32[]{:S(2)}) collective-permute-start(bf16[16,4096]{1,0:T(8,128)(2,1)S(1)} %collective-permute-done.6.refs_7_), channel_id=1, source_target_pairs={{0,8},{8,16},{16,24},{24,28},{28,20},{20,12},{12,4},{4,0},{1,9},{9... | collective-permute-start | bytes 393224 | tf_op jit(solution)/shard_map/ppermute | solution.py:322
  17.0 1.6 %collective-permute-start.21 = (bf16[16,4096]{1,0:T(8,128)(2,1)S(1)}, bf16[16,4096]{1,0:T(8,128)(2,1)S(1)}, u32[]{:S(2)}, u32[]{:S(2)}) collective-permute-start(bf16[16,4096]{1,0:T(8,128)(2,1)S(1)} %get-tuple-element.64.refs_0_), channel_id=1, source_target_pairs={{0,8},{8,16},{16,24},{24,28},{28,20},{20,12},{12,4},{4,0},{1,9},{9... | collective-permute-start | bytes 393224 | tf_op jit(solution)/shard_map/ppermute | solution.py:322
  18.6 0.4 collective-permute-start.18
  19.0 0.5 collective-permute-done.3.refs_1_
  20.0 1.6 %collective-permute-done.7.refs_6_ = bf16[16,4096]{1,0:T(8,128)(2,1)S(1)} collective-permute-done((bf16[16,4096]{1,0:T(8,128)(2,1)S(1)}, bf16[16,4096]{1,0:T(8,128)(2,1)S(1)}, u32[]{:S(2)}, u32[]{:S(2)}) %collective-permute-start.7) | collective-permute-done | bytes 131104 | tf_op jit(solution)/shard_map/ppermute | solution.py:322
  21.6 1.6 %collective-permute-start.8 = (bf16[16,4096]{1,0:T(8,128)(2,1)S(1)}, bf16[16,4096]{1,0:T(8,128)(2,1)S(1)}, u32[]{:S(2)}, u32[]{:S(2)}) collective-permute-start(bf16[16,4096]{1,0:T(8,128)(2,1)S(1)} %collective-permute-done.7.refs_6_), channel_id=1, source_target_pairs={{0,8},{8,16},{16,24},{24,28},{28,20},{20,12},{12,4},{4,0},{1,9},{9... | collective-permute-start | bytes 393224 | tf_op jit(solution)/shard_map/ppermute | solution.py:322
  23.2 1.2 %collective-permute-done.21.refs_7_ = bf16[16,4096]{1,0:T(8,128)(2,1)S(1)} collective-permute-done((bf16[16,4096]{1,0:T(8,128)(2,1)S(1)}, bf16[16,4096]{1,0:T(8,128)(2,1)S(1)}, u32[]{:S(2)}, u32[]{:S(2)}) %collective-permute-start.21) | collective-permute-done | bytes 131104 | tf_op jit(solution)/shard_map/ppermute | solution.py:322
  24.4 1.6 %collective-permute-start.22 = (bf16[16,4096]{1,0:T(8,128)(2,1)S(1)}, bf16[16,4096]{1,0:T(8,128)(2,1)S(1)}, u32[]{:S(2)}, u32[]{:S(2)}) collective-permute-start(bf16[16,4096]{1,0:T(8,128)(2,1)S(1)} %collective-permute-done.21.refs_7_), channel_id=1, source_target_pairs={{0,8},{8,16},{16,24},{24,28},{28,20},{20,12},{12,4},{4,0},{1,9},{9... | collective-permute-start | bytes 393224 | tf_op jit(solution)/shard_map/ppermute | solution.py:322
  26.0 0.5 collective-permute-start.19
  26.5 1.6 %collective-permute-start.5 = (bf16[16,4096]{1,0:T(8,128)(2,1)S(1)}, bf16[16,4096]{1,0:T(8,128)(2,1)S(1)}, u32[]{:S(2)}, u32[]{:S(2)}) collective-permute-start(bf16[16,4096]{1,0:T(8,128)(2,1)S(1)} %collective-permute-done.4.refs_2_), channel_id=1, source_target_pairs={{0,4},{8,0},{16,8},{24,16},{28,24},{20,28},{12,20},{4,12},{1,5},{9... | collective-permute-start | bytes 393224 | tf_op jit(solution)/shard_map/ppermute | solution.py:322
  28.1 0.9 %collective-permute-start.9 = (bf16[16,4096]{1,0:T(8,128)(2,1)S(1)}, bf16[16,4096]{1,0:T(8,128)(2,1)S(1)}, u32[]{:S(2)}, u32[]{:S(2)}) collective-permute-start(bf16[16,4096]{1,0:T(8,128)(2,1)S(1)} %collective-permute-done.8.refs_5_), channel_id=1, source_target_pairs={{0,8},{8,16},{16,24},{24,28},{28,20},{20,12},{12,4},{4,0},{1,9},{9... | collective-permute-start | bytes 393224 | tf_op jit(solution)/shard_map/ppermute | solution.py:322
  28.9 1.9 %collective-permute-done.22.refs_6_ = bf16[16,4096]{1,0:T(8,128)(2,1)S(1)} collective-permute-done((bf16[16,4096]{1,0:T(8,128)(2,1)S(1)}, bf16[16,4096]{1,0:T(8,128)(2,1)S(1)}, u32[]{:S(2)}, u32[]{:S(2)}) %collective-permute-start.22) | collective-permute-done | bytes 131104 | tf_op jit(solution)/shard_map/ppermute | solution.py:322
  30.8 1.6 %collective-permute-start.23 = (bf16[16,4096]{1,0:T(8,128)(2,1)S(1)}, bf16[16,4096]{1,0:T(8,128)(2,1)S(1)}, u32[]{:S(2)}, u32[]{:S(2)}) collective-permute-start(bf16[16,4096]{1,0:T(8,128)(2,1)S(1)} %collective-permute-done.22.refs_6_), channel_id=1, source_target_pairs={{0,8},{8,16},{16,24},{24,28},{28,20},{20,12},{12,4},{4,0},{1,9},{9... | collective-permute-start | bytes 393224 | tf_op jit(solution)/shard_map/ppermute | solution.py:322
  32.4 0.5 collective-permute-start.20
  32.8 3.5 %shard_map.112 = (bf16[4096,256]{1,0:T(8,128)(2,1)S(1)}, bf16[4096,256]{1,0:T(8,128)(2,1)S(1)}, bf16[256,4096]{1,0:T(8,128)(2,1)S(1)}, bf16[256,4096]{1,0:T(8,12...) custom-call(bf16[4096,256]{1,0:T(8,128)(2,1)} %bitcast.13, bf16[4096,256]{1,0:T(8,128)(2,1)} %bitcast.14, ...), custom_call_target="tpu_custom_call" | custom-call | tf_op jit(solution)/shard_map/pallas_call | solution.py:106
  36.3 1.1 %shard_map.113 = (bf16[128,4096]{1,0:T(8,128)(2,1)S(1)}, bf16[128,256]{1,0:T(8,128)(2,1)S(1)}, f32[128,256]{1,0:T(8,128)S(1)}, f32[128,256]{1,0:T(8,128)S(1)}, f...) custom-call(bf16[16,4096]{1,0:T(8,128)(2,1)S(1)} %get-tuple-element., ...), custom_call_target="tpu_custom_call" | custom-call | tf_op jit(solution)/shard_map/pallas_call | solution.py:274
  37.5 1.6 %shard_map.114 = (bf16[128,4096]{1,0:T(8,128)(2,1)S(1)}, bf16[128,256]{1,0:T(8,128)(2,1)S(1)}, bf16[128,256]{1,0:T(8,128)(2,1)S(1)}, f32[16,4096]{1,0:T(8,128)S(...) custom-call(bf16[16,4096]{1,0:T(8,128)(2,1)S(1)} %get-tuple-element., ...), custom_call_target="tpu_custom_call" | custom-call | tf_op jit(solution)/shard_map/pallas_call | solution.py:305
  39.1 1.6 %collective-permute-start.28 = (bf16[16,4096]{1,0:T(8,128)(2,1)S(1)}, bf16[16,4096]{1,0:T(8,128)(2,1)S(1)}, u32[]{:S(2)}, u32[]{:S(2)}) collective-permute-start(bf16[16,4096]{1,0:T(8,128)(2,1)S(1)} %get-tuple-element.75), channel_id=1, source_target_pairs={{0,8},{8,16},{16,24},{24,28},{28,20},{20,12},{12,4},{4,0},{1,9},{9... | collective-permute-start | bytes 393224 | tf_op jit(solution)/shard_map/ppermute | solution.py:322
  41.2 1.6 %collective-permute-start.14 = (bf16[16,4096]{1,0:T(8,128)(2,1)S(1)}, bf16[16,4096]{1,0:T(8,128)(2,1)S(1)}, u32[]{:S(2)}, u32[]{:S(2)}) collective-permute-start(bf16[16,4096]{1,0:T(8,128)(2,1)S(1)} %get-tuple-element.61), channel_id=1, source_target_pairs={{0,4},{8,0},{16,8},{24,16},{28,24},{20,28},{12,20},{4,12},{1,5},{9... | collective-permute-start | bytes 393224 | tf_op jit(solution)/shard_map/ppermute | solution.py:322
  43.2 1.0 %collective-permute-done.28 = bf16[16,4096]{1,0:T(8,128)(2,1)S(1)} collective-permute-done((bf16[16,4096]{1,0:T(8,128)(2,1)S(1)}, bf16[16,4096]{1,0:T(8,128)(2,1)S(1)}, u32[]{:S(2)}, u32[]{:S(2)}) %collective-permute-start.28) | collective-permute-done | bytes 131104 | tf_op jit(solution)/shard_map/ppermute | solution.py:322
  44.2 1.6 %collective-permute-start.29 = (bf16[16,4096]{1,0:T(8,128)(2,1)S(1)}, bf16[16,4096]{1,0:T(8,128)(2,1)S(1)}, u32[]{:S(2)}, u32[]{:S(2)}) collective-permute-start(bf16[16,4096]{1,0:T(8,128)(2,1)S(1)} %add_convert_fusion.1), channel_id=1, source_target_pairs={{0,8},{8,16},{16,24},{24,28},{28,20},{20,12},{12,4},{4,0},{1,9},{9... | collective-permute-start | bytes 393224 | tf_op jit(solution)/shard_map/ppermute | solution.py:322
  45.9 1.1 %collective-permute-done.24 = bf16[16,4096]{1,0:T(8,128)(2,1)S(1)} collective-permute-done((bf16[16,4096]{1,0:T(8,128)(2,1)S(1)}, bf16[16,4096]{1,0:T(8,128)(2,1)S(1)}, u32[]{:S(2)}, u32[]{:S(2)}) %collective-permute-start.24) | collective-permute-done | bytes 131104 | tf_op jit(solution)/shard_map/ppermute | solution.py:322
  47.0 0.5 collective-permute-start.25
  47.5 2.1 %collective-permute-done.14 = bf16[16,4096]{1,0:T(8,128)(2,1)S(1)} collective-permute-done((bf16[16,4096]{1,0:T(8,128)(2,1)S(1)}, bf16[16,4096]{1,0:T(8,128)(2,1)S(1)}, u32[]{:S(2)}, u32[]{:S(2)}) %collective-permute-start.14) | collective-permute-done | bytes 131104 | tf_op jit(solution)/shard_map/ppermute | solution.py:322
  49.7 0.5 collective-permute-start.15
  50.2 1.6 %collective-permute-start.11 = (bf16[16,4096]{1,0:T(8,128)(2,1)S(1)}, bf16[16,4096]{1,0:T(8,128)(2,1)S(1)}, u32[]{:S(2)}, u32[]{:S(2)}) collective-permute-start(bf16[16,4096]{1,0:T(8,128)(2,1)S(1)} %add_convert_fusion.9), channel_id=1, source_target_pairs={{0,8},{8,16},{16,24},{24,28},{28,20},{20,12},{12,4},{4,0},{1,9},{9... | collective-permute-start | bytes 393224 | tf_op jit(solution)/shard_map/ppermute | solution.py:322
  51.9 1.7 %collective-permute-start.30 = (bf16[16,4096]{1,0:T(8,128)(2,1)S(1)}, bf16[16,4096]{1,0:T(8,128)(2,1)S(1)}, u32[]{:S(2)}, u32[]{:S(2)}) collective-permute-start(bf16[16,4096]{1,0:T(8,128)(2,1)S(1)} %add_convert_fusion), channel_id=1, source_target_pairs={{0,8},{8,16},{16,24},{24,28},{28,20},{20,12},{12,4},{4,0},{1,9},{9... | collective-permute-start | bytes 393224 | tf_op jit(solution)/shard_map/ppermute | solution.py:322
  54.1 1.4 %collective-permute-done.15 = bf16[16,4096]{1,0:T(8,128)(2,1)S(1)} collective-permute-done((bf16[16,4096]{1,0:T(8,128)(2,1)S(1)}, bf16[16,4096]{1,0:T(8,128)(2,1)S(1)}, u32[]{:S(2)}, u32[]{:S(2)}) %collective-permute-start.15) | collective-permute-done | bytes 131104 | tf_op jit(solution)/shard_map/ppermute | solution.py:322
  55.4 0.5 collective-permute-start.16
  56.4 1.6 %collective-permute-start.12 = (bf16[16,4096]{1,0:T(8,128)(2,1)S(1)}, bf16[16,4096]{1,0:T(8,128)(2,1)S(1)}, u32[]{:S(2)}, u32[]{:S(2)}) collective-permute-start(bf16[16,4096]{1,0:T(8,128)(2,1)S(1)} %add_convert_fusion.8), channel_id=1, source_target_pairs={{0,8},{8,16},{16,24},{24,28},{28,20},{20,12},{12,4},{4,0},{1,9},{9... | collective-permute-start | bytes 393224 | tf_op jit(solution)/shard_map/ppermute | solution.py:322
  58.0 0.7 collective-permute-done.26
  59.1 2.3 %collective-permute-done.12 = bf16[16,4096]{1,0:T(8,128)(2,1)S(1)} collective-permute-done((bf16[16,4096]{1,0:T(8,128)(2,1)S(1)}, bf16[16,4096]{1,0:T(8,128)(2,1)S(1)}, u32[]{:S(2)}, u32[]{:S(2)}) %collective-permute-start.12) | collective-permute-done | bytes 131104 | tf_op jit(solution)/shard_map/ppermute | solution.py:322
  61.4 1.6 %collective-permute-start.13 = (bf16[16,4096]{1,0:T(8,128)(2,1)S(1)}, bf16[16,4096]{1,0:T(8,128)(2,1)S(1)}, u32[]{:S(2)}, u32[]{:S(2)}) collective-permute-start(bf16[16,4096]{1,0:T(8,128)(2,1)S(1)} %add_convert_fusion.7), channel_id=1, source_target_pairs={{0,8},{8,16},{16,24},{24,28},{28,20},{20,12},{12,4},{4,0},{1,9},{9... | collective-permute-start | bytes 393224 | tf_op jit(solution)/shard_map/ppermute | solution.py:322
  63.1 0.6 collective-permute-done.27.refs_4_
  63.7 2.7 %collective-permute-done.13.refs_1_ = bf16[16,4096]{1,0:T(8,128)(2,1)S(1)} collective-permute-done((bf16[16,4096]{1,0:T(8,128)(2,1)S(1)}, bf16[16,4096]{1,0:T(8,128)(2,1)S(1)}, u32[]{:S(2)}, u32[]{:S(2)}) %collective-permute-start.13) | collective-permute-done | bytes 131104 | tf_op jit(solution)/shard_map/ppermute | solution.py:322
  66.6 1.8 %collective-permute-start.32 = (bf16[8,4096]{1,0:T(8,128)(2,1)S(1)}, bf16[8,4096]{1,0:T(8,128)(2,1)S(1)}, u32[]{:S(2)}, u32[]{:S(2)}) collective-permute-start(bf16[8,4096]{1,0:T(8,128)(2,1)S(1)} %get-tuple-element.80), channel_id=1, source_target_pairs={{0,2},{1,3},{2,0},{3,1},{4,6},{5,7},{6,4},{7,5},{8,10},{9,11},{10,... | collective-permute-start | bytes 196616 | tf_op jit(solution)/shard_map/ppermute | solution.py:372
  68.5 1.7 %shard_map.118 = bf16[256,4096]{1,0:T(8,128)(2,1)} custom-call(bf16[128,256]{1,0:T(8,128)(2,1)S(1)} %get-tuple-element.89.refs_0_, bf16[128,4096]{1,0:T(8,128)(2,1)S(1)} %get-tuple-element.90.refs_1_), custom_call_target="tpu_custom_call" | custom-call | tf_op jit(solution)/shard_map/pallas_call | solution.py:224
  70.1 2.5 %shard_map.117 = (bf16[4096,256]{1,0:T(8,128)(2,1)}, bf16[4096,256]{1,0:T(8,128)(2,1)}) custom-call(bf16[128,4096]{1,0:T(8,128)(2,1)S(1)} %get-tuple-element.84.refs_0_.refs_2_, bf16[128,256]{1,0:T(8,128)(2,1)S(1)} %get-tuple-element.85.refs_1_, bf16[128,4096]{1,0:T(8,128)(2,1)S(1)} %get-tuple-element.84.refs_0_.refs_2_, ...), custom_call_target="tpu_custom_call" | custom-call | tf_op jit(solution)/shard_map/pallas_call | solution.py:224
  72.7 1.8 %shard_map.116 = (bf16[128,4096]{1,0:T(8,128)(2,1)}, bf16[128,4096]{1,0:T(8,128)(2,1)}) custom-call(s32[1]{0:T(128)} %bitcast.rank_ref.refs_0_, s32[2,128]{1,0:T(2,128)S(1)} %bitcast.10, f32[2,128]{1,0:T(2,128)S(1)} %bitcast.12, bf16[8,4096]{1,0:T(8,128)(2,1)S(1)} %get-tuple-element.78.refs_3_, bf16[8,4096]{1,0:T(8,128)(2,1)S(1)} %collective-permute-done.31.refs_4_, ...), custom_call_target="tpu_custom_call" | custom-call | tf_op jit(solution)/shard_map/pallas_call | solution.py:195
  (43 shorter events, 3.2 us)
Async XLA Ops:
  2.5 3.2 %collective-permute-start = (bf16[8,4096]{1,0:T(8,128)(2,1)S(1)}, bf16[8,4096]{1,0:T(8,128)(2,1)S(1)}, u32[]{:S(2)}, u32[]{:S(2)}) collective-permute-start(bf16[8,4096]{1,0:T(8,128)(2,1)S(1)} %get-tuple-element.49), channel_id=1, source_target_pairs={{0,1},{1,0},{2,3},{3,2},{4,5},{5,4},{6,7},{7,6},{8,9},{9,8},{10,11... | collective-permute-start | bytes 196616 | tf_op jit(solution)/shard_map/ppermute | solution.py:372
  3.1 5.3 %collective-permute-start.1 = (bf16[8,4096]{1,0:T(8,128)(2,1)S(1)}, bf16[8,4096]{1,0:T(8,128)(2,1)S(1)}, u32[]{:S(2)}, u32[]{:S(2)}) collective-permute-start(bf16[8,4096]{1,0:T(8,128)(2,1)S(1)} %get-tuple-element.50), channel_id=1, source_target_pairs={{0,2},{1,3},{2,0},{3,1},{4,6},{5,7},{6,4},{7,5},{8,10},{9,11},{10,... | collective-permute-start | bytes 196616 | tf_op jit(solution)/shard_map/ppermute | solution.py:372
  5.7 4.1 %collective-permute-start.2 = (bf16[8,4096]{1,0:T(8,128)(2,1)S(1)}, bf16[8,4096]{1,0:T(8,128)(2,1)S(1)}, u32[]{:S(2)}, u32[]{:S(2)}) collective-permute-start(bf16[8,4096]{1,0:T(8,128)(2,1)S(1)} %get-tuple-element.51), channel_id=1, source_target_pairs={{0,3},{1,2},{2,1},{3,0},{4,7},{5,6},{6,5},{7,4},{8,11},{9,10},{10,... | collective-permute-start | bytes 196616 | tf_op jit(solution)/shard_map/ppermute | solution.py:372
  9.8 5.6 %collective-permute-start.6 = (bf16[16,4096]{1,0:T(8,128)(2,1)S(1)}, bf16[16,4096]{1,0:T(8,128)(2,1)S(1)}, u32[]{:S(2)}, u32[]{:S(2)}) collective-permute-start(bf16[16,4096]{1,0:T(8,128)(2,1)S(1)} %get-tuple-element.52.refs_0_), channel_id=1, source_target_pairs={{0,8},{8,16},{16,24},{24,28},{28,20},{20,12},{12,4},{4,0},{1,9},{9... | collective-permute-start | bytes 393224 | tf_op jit(solution)/shard_map/ppermute | solution.py:322
  11.4 7.1 %collective-permute-start.17 = (bf16[16,4096]{1,0:T(8,128)(2,1)S(1)}, bf16[16,4096]{1,0:T(8,128)(2,1)S(1)}, u32[]{:S(2)}, u32[]{:S(2)}) collective-permute-start(bf16[16,4096]{1,0:T(8,128)(2,1)S(1)} %get-tuple-element.64.refs_0_), channel_id=1, source_target_pairs={{0,4},{8,0},{16,8},{24,16},{28,24},{20,28},{12,20},{4,12},{1,5},{9... | collective-permute-start | bytes 393224 | tf_op jit(solution)/shard_map/ppermute | solution.py:322
  11.9 7.6 %collective-permute-start.3 = (bf16[16,4096]{1,0:T(8,128)(2,1)S(1)}, bf16[16,4096]{1,0:T(8,128)(2,1)S(1)}, u32[]{:S(2)}, u32[]{:S(2)}) collective-permute-start(bf16[16,4096]{1,0:T(8,128)(2,1)S(1)} %get-tuple-element.52.refs_0_), channel_id=1, source_target_pairs={{0,4},{8,0},{16,8},{24,16},{28,24},{20,28},{12,20},{4,12},{1,5},{9... | collective-permute-start | bytes 393224 | tf_op jit(solution)/shard_map/ppermute | solution.py:322
  15.4 6.2 %collective-permute-start.7 = (bf16[16,4096]{1,0:T(8,128)(2,1)S(1)}, bf16[16,4096]{1,0:T(8,128)(2,1)S(1)}, u32[]{:S(2)}, u32[]{:S(2)}) collective-permute-start(bf16[16,4096]{1,0:T(8,128)(2,1)S(1)} %collective-permute-done.6.refs_7_), channel_id=1, source_target_pairs={{0,8},{8,16},{16,24},{24,28},{28,20},{20,12},{12,4},{4,0},{1,9},{9... | collective-permute-start | bytes 393224 | tf_op jit(solution)/shard_map/ppermute | solution.py:322
  17.0 7.4 %collective-permute-start.21 = (bf16[16,4096]{1,0:T(8,128)(2,1)S(1)}, bf16[16,4096]{1,0:T(8,128)(2,1)S(1)}, u32[]{:S(2)}, u32[]{:S(2)}) collective-permute-start(bf16[16,4096]{1,0:T(8,128)(2,1)S(1)} %get-tuple-element.64.refs_0_), channel_id=1, source_target_pairs={{0,8},{8,16},{16,24},{24,28},{28,20},{20,12},{12,4},{4,0},{1,9},{9... | collective-permute-start | bytes 393224 | tf_op jit(solution)/shard_map/ppermute | solution.py:322
  18.6 7.4 %collective-permute-start.18 = (bf16[16,4096]{1,0:T(8,128)(2,1)S(1)}, bf16[16,4096]{1,0:T(8,128)(2,1)S(1)}, u32[]{:S(2)}, u32[]{:S(2)}) collective-permute-start(bf16[16,4096]{1,0:T(8,128)(2,1)S(1)} %collective-permute-done.17.refs_1_), channel_id=1, source_target_pairs={{0,4},{8,0},{16,8},{24,16},{28,24},{20,28},{12,20},{4,12},{1,5},{9... | collective-permute-start | bytes 393224 | tf_op jit(solution)/shard_map/ppermute | solution.py:322
  19.5 6.9 %collective-permute-start.4 = (bf16[16,4096]{1,0:T(8,128)(2,1)S(1)}, bf16[16,4096]{1,0:T(8,128)(2,1)S(1)}, u32[]{:S(2)}, u32[]{:S(2)}) collective-permute-start(bf16[16,4096]{1,0:T(8,128)(2,1)S(1)} %collective-permute-done.3.refs_1_), channel_id=1, source_target_pairs={{0,4},{8,0},{16,8},{24,16},{28,24},{20,28},{12,20},{4,12},{1,5},{9... | collective-permute-start | bytes 393224 | tf_op jit(solution)/shard_map/ppermute | solution.py:322
  21.6 6.4 %collective-permute-start.8 = (bf16[16,4096]{1,0:T(8,128)(2,1)S(1)}, bf16[16,4096]{1,0:T(8,128)(2,1)S(1)}, u32[]{:S(2)}, u32[]{:S(2)}) collective-permute-start(bf16[16,4096]{1,0:T(8,128)(2,1)S(1)} %collective-permute-done.7.refs_6_), channel_id=1, source_target_pairs={{0,8},{8,16},{16,24},{24,28},{28,20},{20,12},{12,4},{4,0},{1,9},{9... | collective-permute-start | bytes 393224 | tf_op jit(solution)/shard_map/ppermute | solution.py:322
  24.4 6.4 %collective-permute-start.22 = (bf16[16,4096]{1,0:T(8,128)(2,1)S(1)}, bf16[16,4096]{1,0:T(8,128)(2,1)S(1)}, u32[]{:S(2)}, u32[]{:S(2)}) collective-permute-start(bf16[16,4096]{1,0:T(8,128)(2,1)S(1)} %collective-permute-done.21.refs_7_), channel_id=1, source_target_pairs={{0,8},{8,16},{16,24},{24,28},{28,20},{20,12},{12,4},{4,0},{1,9},{9... | collective-permute-start | bytes 393224 | tf_op jit(solution)/shard_map/ppermute | solution.py:322
  26.0 6.4 %collective-permute-start.19 = (bf16[16,4096]{1,0:T(8,128)(2,1)S(1)}, bf16[16,4096]{1,0:T(8,128)(2,1)S(1)}, u32[]{:S(2)}, u32[]{:S(2)}) collective-permute-start(bf16[16,4096]{1,0:T(8,128)(2,1)S(1)} %collective-permute-done.18.refs_2_), channel_id=1, source_target_pairs={{0,4},{8,0},{16,8},{24,16},{28,24},{20,28},{12,20},{4,12},{1,5},{9... | collective-permute-start | bytes 393224 | tf_op jit(solution)/shard_map/ppermute | solution.py:322
  26.5 9.9 %collective-permute-start.5 = (bf16[16,4096]{1,0:T(8,128)(2,1)S(1)}, bf16[16,4096]{1,0:T(8,128)(2,1)S(1)}, u32[]{:S(2)}, u32[]{:S(2)}) collective-permute-start(bf16[16,4096]{1,0:T(8,128)(2,1)S(1)} %collective-permute-done.4.refs_2_), channel_id=1, source_target_pairs={{0,4},{8,0},{16,8},{24,16},{28,24},{20,28},{12,20},{4,12},{1,5},{9... | collective-permute-start | bytes 393224 | tf_op jit(solution)/shard_map/ppermute | solution.py:322
  28.1 8.3 %collective-permute-start.9 = (bf16[16,4096]{1,0:T(8,128)(2,1)S(1)}, bf16[16,4096]{1,0:T(8,128)(2,1)S(1)}, u32[]{:S(2)}, u32[]{:S(2)}) collective-permute-start(bf16[16,4096]{1,0:T(8,128)(2,1)S(1)} %collective-permute-done.8.refs_5_), channel_id=1, source_target_pairs={{0,8},{8,16},{16,24},{24,28},{28,20},{20,12},{12,4},{4,0},{1,9},{9... | collective-permute-start | bytes 393224 | tf_op jit(solution)/shard_map/ppermute | solution.py:322
  30.8 6.7 %collective-permute-start.23 = (bf16[16,4096]{1,0:T(8,128)(2,1)S(1)}, bf16[16,4096]{1,0:T(8,128)(2,1)S(1)}, u32[]{:S(2)}, u32[]{:S(2)}) collective-permute-start(bf16[16,4096]{1,0:T(8,128)(2,1)S(1)} %collective-permute-done.22.refs_6_), channel_id=1, source_target_pairs={{0,8},{8,16},{16,24},{24,28},{28,20},{20,12},{12,4},{4,0},{1,9},{9... | collective-permute-start | bytes 393224 | tf_op jit(solution)/shard_map/ppermute | solution.py:322
  32.4 5.1 %collective-permute-start.20 = (bf16[16,4096]{1,0:T(8,128)(2,1)S(1)}, bf16[16,4096]{1,0:T(8,128)(2,1)S(1)}, u32[]{:S(2)}, u32[]{:S(2)}) collective-permute-start(bf16[16,4096]{1,0:T(8,128)(2,1)S(1)} %collective-permute-done.19.refs_3_), channel_id=1, source_target_pairs={{0,4},{8,0},{16,8},{24,16},{28,24},{20,28},{12,20},{4,12},{1,5},{9... | collective-permute-start | bytes 393224 | tf_op jit(solution)/shard_map/ppermute | solution.py:322
  39.1 5.1 %collective-permute-start.28 = (bf16[16,4096]{1,0:T(8,128)(2,1)S(1)}, bf16[16,4096]{1,0:T(8,128)(2,1)S(1)}, u32[]{:S(2)}, u32[]{:S(2)}) collective-permute-start(bf16[16,4096]{1,0:T(8,128)(2,1)S(1)} %get-tuple-element.75), channel_id=1, source_target_pairs={{0,8},{8,16},{16,24},{24,28},{28,20},{20,12},{12,4},{4,0},{1,9},{9... | collective-permute-start | bytes 393224 | tf_op jit(solution)/shard_map/ppermute | solution.py:322
  40.8 6.2 %collective-permute-start.24 = (bf16[16,4096]{1,0:T(8,128)(2,1)S(1)}, bf16[16,4096]{1,0:T(8,128)(2,1)S(1)}, u32[]{:S(2)}, u32[]{:S(2)}) collective-permute-start(bf16[16,4096]{1,0:T(8,128)(2,1)S(1)} %get-tuple-element.71), channel_id=1, source_target_pairs={{0,4},{8,0},{16,8},{24,16},{28,24},{20,28},{12,20},{4,12},{1,5},{9... | collective-permute-start | bytes 393224 | tf_op jit(solution)/shard_map/ppermute | solution.py:322
  41.2 8.5 %collective-permute-start.14 = (bf16[16,4096]{1,0:T(8,128)(2,1)S(1)}, bf16[16,4096]{1,0:T(8,128)(2,1)S(1)}, u32[]{:S(2)}, u32[]{:S(2)}) collective-permute-start(bf16[16,4096]{1,0:T(8,128)(2,1)S(1)} %get-tuple-element.61), channel_id=1, source_target_pairs={{0,4},{8,0},{16,8},{24,16},{28,24},{20,28},{12,20},{4,12},{1,5},{9... | collective-permute-start | bytes 393224 | tf_op jit(solution)/shard_map/ppermute | solution.py:322
  42.8 7.4 %collective-permute-start.10 = (bf16[16,4096]{1,0:T(8,128)(2,1)S(1)}, bf16[16,4096]{1,0:T(8,128)(2,1)S(1)}, u32[]{:S(2)}, u32[]{:S(2)}) collective-permute-start(bf16[16,4096]{1,0:T(8,128)(2,1)S(1)} %get-tuple-element.57), channel_id=1, source_target_pairs={{0,8},{8,16},{16,24},{24,28},{28,20},{20,12},{12,4},{4,0},{1,9},{9... | collective-permute-start | bytes 393224 | tf_op jit(solution)/shard_map/ppermute | solution.py:322
  44.2 7.6 %collective-permute-start.29 = (bf16[16,4096]{1,0:T(8,128)(2,1)S(1)}, bf16[16,4096]{1,0:T(8,128)(2,1)S(1)}, u32[]{:S(2)}, u32[]{:S(2)}) collective-permute-start(bf16[16,4096]{1,0:T(8,128)(2,1)S(1)} %add_convert_fusion.1), channel_id=1, source_target_pairs={{0,8},{8,16},{16,24},{24,28},{28,20},{20,12},{12,4},{4,0},{1,9},{9... | collective-permute-start | bytes 393224 | tf_op jit(solution)/shard_map/ppermute | solution.py:322
  47.0 6.6 %collective-permute-start.25 = (bf16[16,4096]{1,0:T(8,128)(2,1)S(1)}, bf16[16,4096]{1,0:T(8,128)(2,1)S(1)}, u32[]{:S(2)}, u32[]{:S(2)}) collective-permute-start(bf16[16,4096]{1,0:T(8,128)(2,1)S(1)} %add_convert_fusion.4), channel_id=1, source_target_pairs={{0,4},{8,0},{16,8},{24,16},{28,24},{20,28},{12,20},{4,12},{1,5},{9... | collective-permute-start | bytes 393224 | tf_op jit(solution)/shard_map/ppermute | solution.py:322
  49.7 5.7 %collective-permute-start.15 = (bf16[16,4096]{1,0:T(8,128)(2,1)S(1)}, bf16[16,4096]{1,0:T(8,128)(2,1)S(1)}, u32[]{:S(2)}, u32[]{:S(2)}) collective-permute-start(bf16[16,4096]{1,0:T(8,128)(2,1)S(1)} %add_convert_fusion.6), channel_id=1, source_target_pairs={{0,4},{8,0},{16,8},{24,16},{28,24},{20,28},{12,20},{4,12},{1,5},{9... | collective-permute-start | bytes 393224 | tf_op jit(solution)/shard_map/ppermute | solution.py:322
  50.2 6.1 %collective-permute-start.11 = (bf16[16,4096]{1,0:T(8,128)(2,1)S(1)}, bf16[16,4096]{1,0:T(8,128)(2,1)S(1)}, u32[]{:S(2)}, u32[]{:S(2)}) collective-permute-start(bf16[16,4096]{1,0:T(8,128)(2,1)S(1)} %add_convert_fusion.9), channel_id=1, source_target_pairs={{0,8},{8,16},{16,24},{24,28},{28,20},{20,12},{12,4},{4,0},{1,9},{9... | collective-permute-start | bytes 393224 | tf_op jit(solution)/shard_map/ppermute | solution.py:322
  51.9 11.2 %collective-permute-start.30 = (bf16[16,4096]{1,0:T(8,128)(2,1)S(1)}, bf16[16,4096]{1,0:T(8,128)(2,1)S(1)}, u32[]{:S(2)}, u32[]{:S(2)}) collective-permute-start(bf16[16,4096]{1,0:T(8,128)(2,1)S(1)} %add_convert_fusion), channel_id=1, source_target_pairs={{0,8},{8,16},{16,24},{24,28},{28,20},{20,12},{12,4},{4,0},{1,9},{9... | collective-permute-start | bytes 393224 | tf_op jit(solution)/shard_map/ppermute | solution.py:322
  53.6 5.0 %collective-permute-start.26 = (bf16[16,4096]{1,0:T(8,128)(2,1)S(1)}, bf16[16,4096]{1,0:T(8,128)(2,1)S(1)}, u32[]{:S(2)}, u32[]{:S(2)}) collective-permute-start(bf16[16,4096]{1,0:T(8,128)(2,1)S(1)} %add_convert_fusion.3), channel_id=1, source_target_pairs={{0,4},{8,0},{16,8},{24,16},{28,24},{20,28},{12,20},{4,12},{1,5},{9... | collective-permute-start | bytes 393224 | tf_op jit(solution)/shard_map/ppermute | solution.py:322
  55.4 7.6 %collective-permute-start.16 = (bf16[16,4096]{1,0:T(8,128)(2,1)S(1)}, bf16[16,4096]{1,0:T(8,128)(2,1)S(1)}, u32[]{:S(2)}, u32[]{:S(2)}) collective-permute-start(bf16[16,4096]{1,0:T(8,128)(2,1)S(1)} %add_convert_fusion.5), channel_id=1, source_target_pairs={{0,4},{8,0},{16,8},{24,16},{28,24},{20,28},{12,20},{4,12},{1,5},{9... | collective-permute-start | bytes 393224 | tf_op jit(solution)/shard_map/ppermute | solution.py:322
  56.4 5.0 %collective-permute-start.12 = (bf16[16,4096]{1,0:T(8,128)(2,1)S(1)}, bf16[16,4096]{1,0:T(8,128)(2,1)S(1)}, u32[]{:S(2)}, u32[]{:S(2)}) collective-permute-start(bf16[16,4096]{1,0:T(8,128)(2,1)S(1)} %add_convert_fusion.8), channel_id=1, source_target_pairs={{0,8},{8,16},{16,24},{24,28},{28,20},{20,12},{12,4},{4,0},{1,9},{9... | collective-permute-start | bytes 393224 | tf_op jit(solution)/shard_map/ppermute | solution.py:322
  58.7 5.0 %collective-permute-start.27 = (bf16[16,4096]{1,0:T(8,128)(2,1)S(1)}, bf16[16,4096]{1,0:T(8,128)(2,1)S(1)}, u32[]{:S(2)}, u32[]{:S(2)}) collective-permute-start(bf16[16,4096]{1,0:T(8,128)(2,1)S(1)} %add_convert_fusion.2), channel_id=1, source_target_pairs={{0,4},{8,0},{16,8},{24,16},{28,24},{20,28},{12,20},{4,12},{1,5},{9... | collective-permute-start | bytes 393224 | tf_op jit(solution)/shard_map/ppermute | solution.py:322
  61.4 5.0 %collective-permute-start.13 = (bf16[16,4096]{1,0:T(8,128)(2,1)S(1)}, bf16[16,4096]{1,0:T(8,128)(2,1)S(1)}, u32[]{:S(2)}, u32[]{:S(2)}) collective-permute-start(bf16[16,4096]{1,0:T(8,128)(2,1)S(1)} %add_convert_fusion.7), channel_id=1, source_target_pairs={{0,8},{8,16},{16,24},{24,28},{28,20},{20,12},{12,4},{4,0},{1,9},{9... | collective-permute-start | bytes 393224 | tf_op jit(solution)/shard_map/ppermute | solution.py:322
  66.5 6.2 %collective-permute-start.31 = (bf16[8,4096]{1,0:T(8,128)(2,1)S(1)}, bf16[8,4096]{1,0:T(8,128)(2,1)S(1)}, u32[]{:S(2)}, u32[]{:S(2)}) collective-permute-start(bf16[8,4096]{1,0:T(8,128)(2,1)S(1)} %get-tuple-element.79), channel_id=1, source_target_pairs={{0,1},{1,0},{2,3},{3,2},{4,5},{5,4},{6,7},{7,6},{8,9},{9,8},{10,11... | collective-permute-start | bytes 196616 | tf_op jit(solution)/shard_map/ppermute | solution.py:372
  66.6 6.1 %collective-permute-start.32 = (bf16[8,4096]{1,0:T(8,128)(2,1)S(1)}, bf16[8,4096]{1,0:T(8,128)(2,1)S(1)}, u32[]{:S(2)}, u32[]{:S(2)}) collective-permute-start(bf16[8,4096]{1,0:T(8,128)(2,1)S(1)} %get-tuple-element.80), channel_id=1, source_target_pairs={{0,2},{1,3},{2,0},{3,1},{4,6},{5,7},{6,4},{7,5},{8,10},{9,11},{10,... | collective-permute-start | bytes 196616 | tf_op jit(solution)/shard_map/ppermute | solution.py:372
  68.4 4.3 %collective-permute-start.33 = (bf16[8,4096]{1,0:T(8,128)(2,1)S(1)}, bf16[8,4096]{1,0:T(8,128)(2,1)S(1)}, u32[]{:S(2)}, u32[]{:S(2)}) collective-permute-start(bf16[8,4096]{1,0:T(8,128)(2,1)S(1)} %get-tuple-element.81), channel_id=1, source_target_pairs={{0,3},{1,2},{2,1},{3,0},{4,7},{5,6},{6,5},{7,4},{8,11},{9,10},{10,... | collective-permute-start | bytes 196616 | tf_op jit(solution)/shard_map/ppermute | solution.py:372
  68.5 4.3 %copy-start = (s32[128,2]{0,1:T(2,128)S(1)}, s32[128,2]{0,1:T(2,128)}, u32[]{:S(2)}) copy-start(s32[128,2]{0,1:T(2,128)} %param.8) | copy-start | bytes 3076
  68.5 4.3 %copy-start.1 = (f32[128,2]{0,1:T(2,128)S(1)}, f32[128,2]{0,1:T(2,128)}, u32[]{:S(2)}) copy-start(f32[128,2]{0,1:T(2,128)} %param.9) | copy-start | bytes 3076
where the time goes:
time: 74.7 us; the launch traced here: 74.6 us
  starting transfers between devices  35.5 us (48%)
  waiting for transfers between devices  23.7 us (32%)
  Pallas kernels  14.3 us (19%)
  between operations  0.84 us (1%)
    ppermute x28, starting transfers between devices, shift(): return lax.ppermute(value, ('ep', 'rep'), pairs)  30.4 us
    ppermute x28, waiting for transfers between devices, shift(): return lax.ppermute(value, ('ep', 'rep'), pairs)  19.7 us
    ppermute x6, starting transfers between devices, trade(): found.append(lax.ppermute(blocks[k], 'rep', [(i, i ^ k) for i in range(n)]))  5.1 us
    pallas_call x2, Pallas kernels, weight_grads(): pl.pallas_call(body, out_shape=[jax.ShapeDtypeStruct(shape, BF) for shape...  4.2 us
    ppermute x6, waiting for transfers between devices, trade(): found.append(lax.ppermute(blocks[k], 'rep', [(i, i ^ k) for i in range(n)]))  4.03 us
    pallas_call x1, Pallas kernels, load(): pl.pallas_call(body, out_shape=[jax.ShapeDtypeStruct(a.shape, a.dtype) fo...  3.48 us
    pallas_call x1, Pallas kernels, pack(): pl.pallas_call(body, out_shape=[jax.ShapeDtypeStruct((2 * CAP, width), BF...  1.87 us
    pallas_call x1, Pallas kernels, unpack(): return kernel(rank_id, ids, weights, *blocks)  1.81 us
  transfers between devices with their start and end apart: 34, of which 16 were waited for; matrix products, arithmetic and copies ran while one was open for 0% of the time, Pallas kernels for 12%

commit v1 on v0

--- a/solution.py
+++ b/solution.py
@@ -54,12 +54,14 @@
 
 
 def pack(rank_id, ids, weights, tokens, cotangent, n_rep):
-    width = tokens.shape[1]
+    tok, width = tokens.shape
+    slots = n_rep * CAP
     given = [ids, weights, tokens, cotangent]
 
     def body(rank_ref, *refs):
-        ins, outs = refs[:4], refs[4 : 4 + n_rep]
-        held, sems = refs[4 + n_rep : 8 + n_rep], refs[-1]
+        ins, outs = refs[:4], refs[4 : 4 + 2 * n_rep]
+        pick_ref, scale_ref = refs[4 + 2 * n_rep : 6 + 2 * n_rep]
+        held, sems = refs[6 + 2 * n_rep : 10 + 2 * n_rep], refs[-1]
         copies = [
             pltpu.make_async_copy(src, dst, sems.at[i])
             for i, (src, dst) in enumerate(zip(ins, held))
@@ -71,61 +73,58 @@
         chosen, first = selection(rank_ref[0], held[0][...], n_rep)
         scale = slot_weights(chosen, first, held[1][...])
         pick = jnp.where(chosen, 1.0, 0.0).astype(BF)
+        pick_ref[...] = pick
+        scale_ref[...] = jnp.broadcast_to(scale, (slots, tok))
         copies[2].wait()
         rows = jnp.dot(pick, held[2][...], preferred_element_type=F32)
         for k in range(n_rep):
-            outs[k][0:CAP, :] = rows[k * CAP : (k + 1) * CAP].astype(BF)
+            outs[k][...] = rows[k * CAP : (k + 1) * CAP].astype(BF)
         copies[3].wait()
         rows = jnp.dot(pick, held[3][...], preferred_element_type=F32) * scale
         for k in range(n_rep):
-            outs[k][CAP : 2 * CAP, :] = rows[k * CAP : (k + 1) * CAP].astype(BF)
-
-    return pl.pallas_call(
+            outs[n_rep + k][...] = rows[k * CAP : (k + 1) * CAP].astype(BF)
+
+    out = pl.pallas_call(
         body,
-        out_shape=[jax.ShapeDtypeStruct((2 * CAP, width), BF)] * n_rep,
+        out_shape=[jax.ShapeDtypeStruct((CAP, width), BF)] * (2 * n_rep)
+        + [jax.ShapeDtypeStruct((slots, tok), BF), jax.ShapeDtypeStruct((slots, tok), F32)],
         in_specs=[SMEM] + [HBM] * 4,
-        out_specs=[VMEM] * n_rep,
+        out_specs=[VMEM] * (2 * n_rep + 2),
         scratch_shapes=[pltpu.VMEM(v.shape, v.dtype) for v in given]
         + [pltpu.SemaphoreType.DMA((4,))],
         compiler_params=pltpu.CompilerParams(vmem_limit_bytes=12 << 20),
     )(rank_id, *in_hbm(given))
-
-
-def load(*arrays):
-    n = len(arrays)
-
-    def body(*refs):
-        ins, outs, turned, sems = refs[:n], refs[n : 2 * n], refs[2 * n : 3 * n], refs[3 * n]
-        copies = [pltpu.make_async_copy(ins[i], outs[i], sems.at[i]) for i in range(n)]
-        for copy in copies:
-            copy.start()
-        for i in range(n):
-            copies[i].wait()
-            turned[i][...] = outs[i][...].T
-
-    out = pl.pallas_call(
+    return out[:n_rep], out[n_rep : 2 * n_rep], out[-2], out[-1]
+
+
+def load(array):
+    def body(src, dst, turned, sem):
+        copy = pltpu.make_async_copy(src, dst, sem)
+        copy.start()
+        copy.wait()
+        turned[...] = dst[...].T
+
+    return pl.pallas_call(
         body,
-        out_shape=[jax.ShapeDtypeStruct(a.shape, a.dtype) for a in arrays]
-        + [jax.ShapeDtypeStruct(a.shape[::-1], a.dtype) for a in arrays],
-        in_specs=[HBM] * n,
-        out_specs=[VMEM] * (2 * n),
-        scratch_shapes=[pltpu.SemaphoreType.DMA((n,))],
+        out_shape=[
+            jax.ShapeDtypeStruct(array.shape, array.dtype),
+            jax.ShapeDtypeStruct(array.shape[::-1], array.dtype),
+        ],
+        in_specs=[HBM],
+        out_specs=[VMEM] * 2,
+        scratch_shapes=[pltpu.SemaphoreType.DMA],
         compiler_params=pltpu.CompilerParams(vmem_limit_bytes=12 << 20),
-    )(*in_hbm(arrays))
-    return out[:n], out[n:]
-
-
-def split(blocks):
+    )(*in_hbm([array]))
+
+
+def join(blocks):
     n = len(blocks)
     width = blocks[0].shape[1]
 
     def body(*refs):
-        ins, (tok_ref, up_ref) = refs[:n], refs[n:]
-        tok_ref[...] = jnp.concatenate([r[0:CAP, :] for r in ins], axis=0)
-        up_ref[...] = jnp.concatenate([r[CAP : 2 * CAP, :] for r in ins], axis=0)
-
-    shape = [jax.ShapeDtypeStruct((n * CAP, width), BF)] * 2
-    return call(body, shape, n)(*blocks)
+        refs[n][...] = jnp.concatenate([r[...] for r in refs[:n]], axis=0)
+
+    return call(body, jax.ShapeDtypeStruct((n * CAP, width), BF), n)(*blocks)
 
 
 def streamed(compute, tiles, out_shapes, n_in, smem=0):
@@ -162,37 +161,33 @@
 OVER_ROWS = (((0,), (0,)), ((), ()))
 
 
-def unpack(rank_id, ids, weights, blocks):
+def unpack(pick, scale, blocks):
     n = len(blocks)
     width = blocks[0].shape[1]
-    tok = ids.shape[1]
+    tok = pick.shape[1]
+    lead = [pick] if scale is None else [pick, scale]
     tiles = 4
     cols = width // tiles
 
     def compute(ins, i, state):
         at = slice(i * cols, (i + 1) * cols)
-        if state is None:
-            chosen, first = selection(ins[0][0], ins[1][...], n)
-            pick = jnp.where(chosen, 1.0, 0.0).astype(BF)
-            state = (pick, slot_weights(chosen, first, ins[2][...]))
-        pick, scale = state
-        full = jnp.concatenate([r[0:CAP, at].astype(F32) for r in ins[3:]], axis=0) * scale
-        top = full.astype(BF)
-        rest = full - top.astype(F32)
-        middle = rest.astype(BF)
-        low = (rest - middle.astype(F32)).astype(BF)
-        mixed = lax.dot_general(
-            jnp.concatenate([pick, pick, pick], axis=0),
-            jnp.concatenate([top, middle, low], axis=0),
-            OVER_ROWS,
-            preferred_element_type=F32,
-        )
-        rows = jnp.concatenate([r[CAP : 2 * CAP, at] for r in ins[3:]], axis=0)
-        grads = lax.dot_general(pick, rows, OVER_ROWS, preferred_element_type=F32)
-        return state, [((slice(None), at), mixed), ((slice(None), at), grads)]
-
-    kernel = streamed(compute, tiles, [(tok, width)] * 2, 3 + n, smem=1)
-    return kernel(rank_id, ids, weights, *blocks)
+        chosen = ins[0][...]
+        parts = [r[:, at] for r in ins[len(lead) :]]
+        if scale is None:
+            rows = jnp.concatenate(parts, axis=0)
+        else:
+            full = jnp.concatenate([p.astype(F32) for p in parts], axis=0) * ins[1][:, 0:1]
+            top = full.astype(BF)
+            rest = full - top.astype(F32)
+            middle = rest.astype(BF)
+            low = (rest - middle.astype(F32)).astype(BF)
+            rows = jnp.concatenate([top, middle, low], axis=0)
+            chosen = jnp.concatenate([chosen, chosen, chosen], axis=0)
+        value = lax.dot_general(chosen, rows, OVER_ROWS, preferred_element_type=F32)
+        return state, [((slice(None), at), value)]
+
+    kernel = streamed(compute, tiles, [(tok, width)], len(lead) + n)
+    return kernel(*lead, *blocks)[0]
 
 
 def weight_grads(*jobs):
@@ -350,19 +345,16 @@
     return parts[0], ahead, behind
 
 
-def finish(routed, row_grads, n):
-    width = routed[0].shape[1]
-
-    def body(*refs):
-        ins, outs = refs[:6], refs[6:]
-        for half in range(2):
-            own, ahead, behind = ins[3 * half : 3 * half + 3]
-            total = own[...] + ahead[...].astype(F32) + behind[...].astype(F32)
-            for k in range(n):
-                outs[k][half * CAP : (half + 1) * CAP, :] = total[k * CAP : (k + 1) * CAP].astype(BF)
-
-    shape = [jax.ShapeDtypeStruct((2 * CAP, width), BF)] * n
-    return call(body, shape, 6)(*routed, *row_grads)
+def finish(own, ahead, behind, n):
+    width = own.shape[1]
+
+    def body(own_ref, ahead_ref, behind_ref, *outs):
+        total = own_ref[...] + ahead_ref[...].astype(F32) + behind_ref[...].astype(F32)
+        for k in range(n):
+            outs[k][...] = total[k * CAP : (k + 1) * CAP].astype(BF)
+
+    shape = [jax.ShapeDtypeStruct((CAP, width), BF)] * n
+    return call(body, shape, 3)(own, ahead, behind)
 
 
 def trade(blocks):
@@ -379,9 +371,13 @@
     ids = expert_ids.T
     weights = route_weights.T
 
-    sent = pack(rank_id, ids, weights, tokens, cotangent, n_rep)
-    token_rows, up_rows = split(trade(sent))
-    plain, turned = load(w_gate[0], w_up[0], w_down[0])
+    sent, sent_ups, pick, scale = pack(rank_id, ids, weights, tokens, cotangent, n_rep)
+    token_rows = join(trade(sent))
+    up_rows = join(trade(sent_ups))
+    wg, wg_turned = load(w_gate[0])
+    wu, wu_turned = load(w_up[0])
+    wd, wd_turned = load(w_down[0])
+    plain, turned = (wg, wu, wd), (wg_turned, wu_turned, wd_turned)
     token_chunks = ring_gather(token_rows, 1)
     up_chunks = ring_gather(up_rows, -1)
     all_tokens, hidden, activated, slope, routed_parts = forward(token_chunks, *plain, 1)
@@ -390,8 +386,10 @@
     row_grads = ring_scatter(grad_parts, -1)
     grad_gate, grad_up = weight_grads((all_tokens, d_gate), (all_tokens, d_up))
     (grad_down,) = weight_grads((hidden, all_ups))
-    back = trade(finish(routed, row_grads, n_rep))
-    mixed, grad_tokens = unpack(rank_id, ids, weights, back)
+    back = trade(finish(*routed, n_rep))
+    mixed = unpack(pick, scale, back)
+    back = trade(finish(*row_grads, n_rep))
+    grad_tokens = unpack(pick, None, back)
     return (mixed, grad_tokens, grad_gate[None], grad_up[None], grad_down[None])
 
 

time: 74.7 us -> 77.7 us (1.040)
  waiting for transfers between devices: 23.7 us -> 16.1 us
  starting transfers between devices: 35.5 us -> 42 us
  Pallas kernels: 14.3 us -> 18.2 us
    ppermute x28, waiting for transfers between devices: 19.7 us -> 14.2 us  [shift(): return lax.ppermute(value, ('ep', 'rep'), pairs)]
    ppermute x6 -> x12, starting transfers between devices: 5.1 us -> 9.11 us  [trade(): found.append(lax.ppermute(blocks[k], 'rep', [(i, i ^ k) for i in range(n)]))]
    pallas_call x5 -> x10, Pallas kernels: 7.34 us -> 11.3 us  [the longest x3 6.67 us: load(): pl.pallas_call(body, out_shape=[jax.ShapeDtypeStruct(array.shape, array.d...]
    ppermute x28, starting transfers between devices: 30.4 us -> 32.8 us  [shift(): return lax.ppermute(value, ('ep', 'rep'), pairs)]
    ppermute x6 -> x12, waiting for transfers between devices: 4.03 us -> 1.97 us  [trade(): found.append(lax.ppermute(blocks[k], 'rep', [(i, i ^ k) for i in range(n)]))]
  transfers between devices with their start and end apart: 34 -> 40, of which waited for: 16 -> 14; matrix products, arithmetic and copies ran while one was open for 0% -> 0% of each run, Pallas kernels for 12% -> 17%
where the time goes in v1:
time: 77.7 us; the launch traced here: 77.5 us
  starting transfers between devices  42 us (54%)
  Pallas kernels  18.2 us (23%)
  waiting for transfers between devices  16.1 us (21%)
  between operations  0.89 us (1%)
    ppermute x28, starting transfers between devices, shift(): return lax.ppermute(value, ('ep', 'rep'), pairs)  32.8 us
    ppermute x28, waiting for transfers between devices, shift(): return lax.ppermute(value, ('ep', 'rep'), pairs)  14.2 us
    ppermute x12, starting transfers between devices, trade(): found.append(lax.ppermute(blocks[k], 'rep', [(i, i ^ k) for i in range(n)]))  9.11 us
    pallas_call x3, Pallas kernels, load(): pl.pallas_call(body, out_shape=[jax.ShapeDtypeStruct(array.shape, array.d...  6.67 us
    pallas_call x2, Pallas kernels, weight_grads(): pl.pallas_call(body, out_shape=[jax.ShapeDtypeStruct(shape, BF) for shape...  4.2 us
    pallas_call x2, Pallas kernels, unpack(): return kernel(*lead, *blocks)[0]  2.53 us
    ppermute x12, waiting for transfers between devices, trade(): found.append(lax.ppermute(blocks[k], 'rep', [(i, i ^ k) for i in range(n)]))  1.97 us
    pallas_call x1, Pallas kernels, pack(): pl.pallas_call(body, out_shape=[jax.ShapeDtypeStruct((CAP, width), BF)] *...  1.87 us
  transfers between devices with their start and end apart: 40, of which 14 were waited for; matrix products, arithmetic and copies ran while one was open for 0% of the time, Pallas kernels for 17%

profile of v1, /device:TPU:0, one launch (start us, length us, event | category | flops | bytes accessed | tf_op | source)
XLA Modules:
  0.0 77.5 jit_solution(1297393622865735381)
XLA Ops:
  0.6 1.9 %shard_map.110 = (bf16[4,4096]{1,0:T(4,128)(2,1)S(1)}, bf16[4,4096]{1,0:T(4,128)(2,1)S(1)}, bf16[4,4096]{1,0:T(4,128)(2,1)S(1)}, bf16[4,4096]{1,0:T(4,128)(2,1)S...) custom-call(s32[1]{0:T(128)} %bitcast.rank_ref, ...), custom_call_target="tpu_custom_call" | custom-call | tf_op jit(solution)/shard_map/pallas_call | solution.py:87
  2.5 0.6 collective-permute-start
  3.1 2.6 %collective-permute-start.1 = (bf16[4,4096]{1,0:T(4,128)(2,1)S(1)}, bf16[4,4096]{1,0:T(4,128)(2,1)S(1)}, u32[]{:S(2)}, u32[]{:S(2)}) collective-permute-start(bf16[4,4096]{1,0:T(4,128)(2,1)S(1)} %get-tuple-element.58), channel_id=1, source_target_pairs={{0,2},{1,3},{2,0},{3,1},{4,6},{5,7},{6,4},{7,5},{8,10},{9,11},{10,... | collective-permute-start | bytes 98312 | tf_op jit(solution)/shard_map/ppermute | solution.py:364
  5.8 1.9 %collective-permute-start.21 = (bf16[4,4096]{1,0:T(4,128)(2,1)S(1)}, bf16[4,4096]{1,0:T(4,128)(2,1)S(1)}, u32[]{:S(2)}, u32[]{:S(2)}) collective-permute-start(bf16[4,4096]{1,0:T(4,128)(2,1)S(1)} %get-tuple-element.77), channel_id=1, source_target_pairs={{0,2},{1,3},{2,0},{3,1},{4,6},{5,7},{6,4},{7,5},{8,10},{9,11},{10,... | collective-permute-start | bytes 98312 | tf_op jit(solution)/shard_map/ppermute | solution.py:364
  7.8 1.2 %collective-permute-done.2.refs_3_ = bf16[4,4096]{1,0:T(4,128)(2,1)S(1)} collective-permute-done((bf16[4,4096]{1,0:T(4,128)(2,1)S(1)}, bf16[4,4096]{1,0:T(4,128)(2,1)S(1)}, u32[]{:S(2)}, u32[]{:S(2)}) %collective-permute-start.2) | collective-permute-done | bytes 32800 | tf_op jit(solution)/shard_map/ppermute | solution.py:364
  9.1 1.6 %collective-permute-start.6 = (bf16[16,4096]{1,0:T(8,128)(2,1)S(1)}, bf16[16,4096]{1,0:T(8,128)(2,1)S(1)}, u32[]{:S(2)}, u32[]{:S(2)}) collective-permute-start(bf16[16,4096]{1,0:T(8,128)(2,1)S(1)} %shard_map.111.refs_0_), channel_id=1, source_target_pairs={{0,8},{8,16},{16,24},{24,28},{28,20},{20,12},{12,4},{4,0},{1,9},{9... | collective-permute-start | bytes 393224 | tf_op jit(solution)/shard_map/ppermute | solution.py:317
  10.7 0.7 collective-permute-done.22.refs_3_
  11.5 1.5 %collective-permute-start.23 = (bf16[16,4096]{1,0:T(8,128)(2,1)S(1)}, bf16[16,4096]{1,0:T(8,128)(2,1)S(1)}, u32[]{:S(2)}, u32[]{:S(2)}) collective-permute-start(bf16[16,4096]{1,0:T(8,128)(2,1)S(1)} %shard_map.118.refs_0_), channel_id=1, source_target_pairs={{0,4},{8,0},{16,8},{24,16},{28,24},{20,28},{12,20},{4,12},{1,5},{9... | collective-permute-start | bytes 393224 | tf_op jit(solution)/shard_map/ppermute | solution.py:317
  13.0 1.6 %collective-permute-start.3 = (bf16[16,4096]{1,0:T(8,128)(2,1)S(1)}, bf16[16,4096]{1,0:T(8,128)(2,1)S(1)}, u32[]{:S(2)}, u32[]{:S(2)}) collective-permute-start(bf16[16,4096]{1,0:T(8,128)(2,1)S(1)} %shard_map.111.refs_0_), channel_id=1, source_target_pairs={{0,4},{8,0},{16,8},{24,16},{28,24},{20,28},{12,20},{4,12},{1,5},{9... | collective-permute-start | bytes 393224 | tf_op jit(solution)/shard_map/ppermute | solution.py:317
  15.0 1.6 %collective-permute-start.7 = (bf16[16,4096]{1,0:T(8,128)(2,1)S(1)}, bf16[16,4096]{1,0:T(8,128)(2,1)S(1)}, u32[]{:S(2)}, u32[]{:S(2)}) collective-permute-start(bf16[16,4096]{1,0:T(8,128)(2,1)S(1)} %collective-permute-done.6.refs_7_), channel_id=1, source_target_pairs={{0,8},{8,16},{16,24},{24,28},{28,20},{20,12},{12,4},{4,0},{1,9},{9... | collective-permute-start | bytes 393224 | tf_op jit(solution)/shard_map/ppermute | solution.py:317
  16.6 1.6 %collective-permute-start.27 = (bf16[16,4096]{1,0:T(8,128)(2,1)S(1)}, bf16[16,4096]{1,0:T(8,128)(2,1)S(1)}, u32[]{:S(2)}, u32[]{:S(2)}) collective-permute-start(bf16[16,4096]{1,0:T(8,128)(2,1)S(1)} %shard_map.118.refs_0_), channel_id=1, source_target_pairs={{0,8},{8,16},{16,24},{24,28},{28,20},{20,12},{12,4},{4,0},{1,9},{9... | collective-permute-start | bytes 393224 | tf_op jit(solution)/shard_map/ppermute | solution.py:317
  18.1 1.2 %collective-permute-start.24 = (bf16[16,4096]{1,0:T(8,128)(2,1)S(1)}, bf16[16,4096]{1,0:T(8,128)(2,1)S(1)}, u32[]{:S(2)}, u32[]{:S(2)}) collective-permute-start(bf16[16,4096]{1,0:T(8,128)(2,1)S(1)} %collective-permute-done.23.refs_1_), channel_id=1, source_target_pairs={{0,4},{8,0},{16,8},{24,16},{28,24},{20,28},{12,20},{4,12},{1,5},{9... | collective-permute-start | bytes 393224 | tf_op jit(solution)/shard_map/ppermute | solution.py:317
  19.4 0.5 collective-permute-done.3.refs_1_
  19.9 2.3 %collective-permute-start.4 = (bf16[16,4096]{1,0:T(8,128)(2,1)S(1)}, bf16[16,4096]{1,0:T(8,128)(2,1)S(1)}, u32[]{:S(2)}, u32[]{:S(2)}) collective-permute-start(bf16[16,4096]{1,0:T(8,128)(2,1)S(1)} %collective-permute-done.3.refs_1_), channel_id=1, source_target_pairs={{0,4},{8,0},{16,8},{24,16},{28,24},{20,28},{12,20},{4,12},{1,5},{9... | collective-permute-start | bytes 393224 | tf_op jit(solution)/shard_map/ppermute | solution.py:317
  22.2 0.7 collective-permute-start.8
  22.9 2.4 %collective-permute-start.28 = (bf16[16,4096]{1,0:T(8,128)(2,1)S(1)}, bf16[16,4096]{1,0:T(8,128)(2,1)S(1)}, u32[]{:S(2)}, u32[]{:S(2)}) collective-permute-start(bf16[16,4096]{1,0:T(8,128)(2,1)S(1)} %collective-permute-done.27.refs_7_), channel_id=1, source_target_pairs={{0,8},{8,16},{16,24},{24,28},{28,20},{20,12},{12,4},{4,0},{1,9},{9... | collective-permute-start | bytes 393224 | tf_op jit(solution)/shard_map/ppermute | solution.py:317
  25.5 0.8 %collective-permute-done.4.refs_2_ = bf16[16,4096]{1,0:T(8,128)(2,1)S(1)} collective-permute-done((bf16[16,4096]{1,0:T(8,128)(2,1)S(1)}, bf16[16,4096]{1,0:T(8,128)(2,1)S(1)}, u32[]{:S(2)}, u32[]{:S(2)}) %collective-permute-start.4) | collective-permute-done | bytes 131104 | tf_op jit(solution)/shard_map/ppermute | solution.py:317
  26.4 2.0 %collective-permute-start.5 = (bf16[16,4096]{1,0:T(8,128)(2,1)S(1)}, bf16[16,4096]{1,0:T(8,128)(2,1)S(1)}, u32[]{:S(2)}, u32[]{:S(2)}) collective-permute-start(bf16[16,4096]{1,0:T(8,128)(2,1)S(1)} %collective-permute-done.4.refs_2_), channel_id=1, source_target_pairs={{0,4},{8,0},{16,8},{24,16},{28,24},{20,28},{12,20},{4,12},{1,5},{9... | collective-permute-start | bytes 393224 | tf_op jit(solution)/shard_map/ppermute | solution.py:317
  28.6 0.6 collective-permute-done.28.refs_6_
  29.2 2.4 %collective-permute-start.29 = (bf16[16,4096]{1,0:T(8,128)(2,1)S(1)}, bf16[16,4096]{1,0:T(8,128)(2,1)S(1)}, u32[]{:S(2)}, u32[]{:S(2)}) collective-permute-start(bf16[16,4096]{1,0:T(8,128)(2,1)S(1)} %collective-permute-done.28.refs_6_), channel_id=1, source_target_pairs={{0,8},{8,16},{16,24},{24,28},{28,20},{20,12},{12,4},{4,0},{1,9},{9... | collective-permute-start | bytes 393224 | tf_op jit(solution)/shard_map/ppermute | solution.py:317
  31.6 2.2 %shard_map.112 = (bf16[4096,256]{1,0:T(8,128)(2,1)S(1)}, bf16[256,4096]{1,0:T(8,128)(2,1)S(1)}) custom-call(bf16[4096,256]{1,0:T(8,128)(2,1)} %bitcast.9), custom_call_target="tpu_custom_call" | custom-call | tf_op jit(solution)/shard_map/pallas_call | solution.py:107
  33.9 2.2 %shard_map.113 = (bf16[4096,256]{1,0:T(8,128)(2,1)S(1)}, bf16[256,4096]{1,0:T(8,128)(2,1)S(1)}) custom-call(bf16[4096,256]{1,0:T(8,128)(2,1)} %bitcast.10), custom_call_target="tpu_custom_call" | custom-call | tf_op jit(solution)/shard_map/pallas_call | solution.py:107
  36.1 2.2 %shard_map.114 = (bf16[256,4096]{1,0:T(8,128)(2,1)S(1)}, bf16[4096,256]{1,0:T(8,128)(2,1)S(1)}) custom-call(bf16[256,4096]{1,0:T(8,128)(2,1)} %bitcast.11), custom_call_target="tpu_custom_call" | custom-call | tf_op jit(solution)/shard_map/pallas_call | solution.py:107
  38.3 1.1 %shard_map.115 = (bf16[128,4096]{1,0:T(8,128)(2,1)S(1)}, bf16[128,256]{1,0:T(8,128)(2,1)S(1)}, f32[128,256]{1,0:T(8,128)S(1)}, f32[128,256]{1,0:T(8,128)S(1)}, f...) custom-call(bf16[16,4096]{1,0:T(8,128)(2,1)S(1)} %shard_map.111.refs, ...), custom_call_target="tpu_custom_call" | custom-call | tf_op jit(solution)/shard_map/pallas_call | solution.py:269
  39.5 1.6 %shard_map.119 = (bf16[128,4096]{1,0:T(8,128)(2,1)S(1)}, bf16[128,256]{1,0:T(8,128)(2,1)S(1)}, bf16[128,256]{1,0:T(8,128)(2,1)S(1)}, f32[16,4096]{1,0:T(8,128)S(...) custom-call(bf16[16,4096]{1,0:T(8,128)(2,1)S(1)} %shard_map.118.refs, ...), custom_call_target="tpu_custom_call" | custom-call | tf_op jit(solution)/shard_map/pallas_call | solution.py:300
  41.1 2.1 %collective-permute-start.34 = (bf16[16,4096]{1,0:T(8,128)(2,1)S(1)}, bf16[16,4096]{1,0:T(8,128)(2,1)S(1)}, u32[]{:S(2)}, u32[]{:S(2)}) collective-permute-start(bf16[16,4096]{1,0:T(8,128)(2,1)S(1)} %get-tuple-element.89), channel_id=1, source_target_pairs={{0,8},{8,16},{16,24},{24,28},{28,20},{20,12},{12,4},{4,0},{1,9},{9... | collective-permute-start | bytes 393224 | tf_op jit(solution)/shard_map/ppermute | solution.py:317
  43.2 1.4 %collective-permute-start.14 = (bf16[16,4096]{1,0:T(8,128)(2,1)S(1)}, bf16[16,4096]{1,0:T(8,128)(2,1)S(1)}, u32[]{:S(2)}, u32[]{:S(2)}) collective-permute-start(bf16[16,4096]{1,0:T(8,128)(2,1)S(1)} %get-tuple-element.68), channel_id=1, source_target_pairs={{0,4},{8,0},{16,8},{24,16},{28,24},{20,28},{12,20},{4,12},{1,5},{9... | collective-permute-start | bytes 393224 | tf_op jit(solution)/shard_map/ppermute | solution.py:317
  44.7 0.6 collective-permute-start.10
  45.3 2.3 %collective-permute-done.34 = bf16[16,4096]{1,0:T(8,128)(2,1)S(1)} collective-permute-done((bf16[16,4096]{1,0:T(8,128)(2,1)S(1)}, bf16[16,4096]{1,0:T(8,128)(2,1)S(1)}, u32[]{:S(2)}, u32[]{:S(2)}) %collective-permute-start.34) | collective-permute-done | bytes 131104 | tf_op jit(solution)/shard_map/ppermute | solution.py:317
  47.6 0.9 %collective-permute-start.35 = (bf16[16,4096]{1,0:T(8,128)(2,1)S(1)}, bf16[16,4096]{1,0:T(8,128)(2,1)S(1)}, u32[]{:S(2)}, u32[]{:S(2)}) collective-permute-start(bf16[16,4096]{1,0:T(8,128)(2,1)S(1)} %add_convert_fusion.1), channel_id=1, source_target_pairs={{0,8},{8,16},{16,24},{24,28},{28,20},{20,12},{12,4},{4,0},{1,9},{9... | collective-permute-start | bytes 393224 | tf_op jit(solution)/shard_map/ppermute | solution.py:317
  48.5 1.1 %collective-permute-done.30 = bf16[16,4096]{1,0:T(8,128)(2,1)S(1)} collective-permute-done((bf16[16,4096]{1,0:T(8,128)(2,1)S(1)}, bf16[16,4096]{1,0:T(8,128)(2,1)S(1)}, u32[]{:S(2)}, u32[]{:S(2)}) %collective-permute-start.30) | collective-permute-done | bytes 131104 | tf_op jit(solution)/shard_map/ppermute | solution.py:317
  49.8 1.8 %collective-permute-done.14 = bf16[16,4096]{1,0:T(8,128)(2,1)S(1)} collective-permute-done((bf16[16,4096]{1,0:T(8,128)(2,1)S(1)}, bf16[16,4096]{1,0:T(8,128)(2,1)S(1)}, u32[]{:S(2)}, u32[]{:S(2)}) %collective-permute-start.14) | collective-permute-done | bytes 131104 | tf_op jit(solution)/shard_map/ppermute | solution.py:317
  52.0 2.0 %collective-permute-start.11 = (bf16[16,4096]{1,0:T(8,128)(2,1)S(1)}, bf16[16,4096]{1,0:T(8,128)(2,1)S(1)}, u32[]{:S(2)}, u32[]{:S(2)}) collective-permute-start(bf16[16,4096]{1,0:T(8,128)(2,1)S(1)} %add_convert_fusion.9), channel_id=1, source_target_pairs={{0,8},{8,16},{16,24},{24,28},{28,20},{20,12},{12,4},{4,0},{1,9},{9... | collective-permute-start | bytes 393224 | tf_op jit(solution)/shard_map/ppermute | solution.py:317
  54.0 2.1 %collective-permute-start.36 = (bf16[16,4096]{1,0:T(8,128)(2,1)S(1)}, bf16[16,4096]{1,0:T(8,128)(2,1)S(1)}, u32[]{:S(2)}, u32[]{:S(2)}) collective-permute-start(bf16[16,4096]{1,0:T(8,128)(2,1)S(1)} %add_convert_fusion), channel_id=1, source_target_pairs={{0,8},{8,16},{16,24},{24,28},{28,20},{20,12},{12,4},{4,0},{1,9},{9... | collective-permute-start | bytes 393224 | tf_op jit(solution)/shard_map/ppermute | solution.py:317
  56.2 1.8 %collective-permute-done.15 = bf16[16,4096]{1,0:T(8,128)(2,1)S(1)} collective-permute-done((bf16[16,4096]{1,0:T(8,128)(2,1)S(1)}, bf16[16,4096]{1,0:T(8,128)(2,1)S(1)}, u32[]{:S(2)}, u32[]{:S(2)}) %collective-permute-start.15) | collective-permute-done | bytes 131104 | tf_op jit(solution)/shard_map/ppermute | solution.py:317
  58.0 0.5 collective-permute-start.16
  58.6 1.6 %collective-permute-start.12 = (bf16[16,4096]{1,0:T(8,128)(2,1)S(1)}, bf16[16,4096]{1,0:T(8,128)(2,1)S(1)}, u32[]{:S(2)}, u32[]{:S(2)}) collective-permute-start(bf16[16,4096]{1,0:T(8,128)(2,1)S(1)} %add_convert_fusion.8), channel_id=1, source_target_pairs={{0,8},{8,16},{16,24},{24,28},{28,20},{20,12},{12,4},{4,0},{1,9},{9... | collective-permute-start | bytes 393224 | tf_op jit(solution)/shard_map/ppermute | solution.py:317
  60.2 0.9 %collective-permute-done.32 = bf16[16,4096]{1,0:T(8,128)(2,1)S(1)} collective-permute-done((bf16[16,4096]{1,0:T(8,128)(2,1)S(1)}, bf16[16,4096]{1,0:T(8,128)(2,1)S(1)}, u32[]{:S(2)}, u32[]{:S(2)}) %collective-permute-start.32) | collective-permute-done | bytes 131104 | tf_op jit(solution)/shard_map/ppermute | solution.py:317
  61.2 2.4 %collective-permute-done.12 = bf16[16,4096]{1,0:T(8,128)(2,1)S(1)} collective-permute-done((bf16[16,4096]{1,0:T(8,128)(2,1)S(1)}, bf16[16,4096]{1,0:T(8,128)(2,1)S(1)}, u32[]{:S(2)}, u32[]{:S(2)}) %collective-permute-start.12) | collective-permute-done | bytes 131104 | tf_op jit(solution)/shard_map/ppermute | solution.py:317
  63.7 1.6 %collective-permute-start.13 = (bf16[16,4096]{1,0:T(8,128)(2,1)S(1)}, bf16[16,4096]{1,0:T(8,128)(2,1)S(1)}, u32[]{:S(2)}, u32[]{:S(2)}) collective-permute-start(bf16[16,4096]{1,0:T(8,128)(2,1)S(1)} %add_convert_fusion.7), channel_id=1, source_target_pairs={{0,8},{8,16},{16,24},{24,28},{28,20},{20,12},{12,4},{4,0},{1,9},{9... | collective-permute-start | bytes 393224 | tf_op jit(solution)/shard_map/ppermute | solution.py:317
  65.3 0.9 %collective-permute-done.33.ahead_ref = bf16[16,4096]{1,0:T(8,128)(2,1)S(1)} collective-permute-done((bf16[16,4096]{1,0:T(8,128)(2,1)S(1)}, bf16[16,4096]{1,0:T(8,128)(2,1)S(1)}, u32[]{:S(2)}, u32[]{:S(2)}) %collective-permute-start.33) | collective-permute-done | bytes 131104 | tf_op jit(solution)/shard_map/ppermute | solution.py:317
  66.4 1.8 %collective-permute-start.39 = (bf16[4,4096]{1,0:T(4,128)(2,1)S(1)}, bf16[4,4096]{1,0:T(4,128)(2,1)S(1)}, u32[]{:S(2)}, u32[]{:S(2)}) collective-permute-start(bf16[4,4096]{1,0:T(4,128)(2,1)S(1)} %get-tuple-element.95), channel_id=1, source_target_pairs={{0,3},{1,2},{2,1},{3,0},{4,7},{5,6},{6,5},{7,4},{8,11},{9,10},{10,... | collective-permute-start | bytes 98312 | tf_op jit(solution)/shard_map/ppermute | solution.py:364
  68.8 0.5 collective-permute-start.18
  69.4 1.3 %collective-permute-start.19 = (bf16[4,4096]{1,0:T(4,128)(2,1)S(1)}, bf16[4,4096]{1,0:T(4,128)(2,1)S(1)}, u32[]{:S(2)}, u32[]{:S(2)}) collective-permute-start(bf16[4,4096]{1,0:T(4,128)(2,1)S(1)} %get-tuple-element.74), channel_id=1, source_target_pairs={{0,3},{1,2},{2,1},{3,0},{4,7},{5,6},{6,5},{7,4},{8,11},{9,10},{10,... | collective-permute-start | bytes 98312 | tf_op jit(solution)/shard_map/ppermute | solution.py:364
  70.7 1.7 %shard_map.123 = bf16[256,4096]{1,0:T(8,128)(2,1)} custom-call(bf16[128,256]{1,0:T(8,128)(2,1)S(1)} %get-tuple-element.101.refs_0_, bf16[128,4096]{1,0:T(8,128)(2,1)S(1)} %get-tuple-element.102.refs_1_), custom_call_target="tpu_custom_call" | custom-call | tf_op jit(solution)/shard_map/pallas_call | solution.py:219
  72.3 2.5 %shard_map.122 = (bf16[4096,256]{1,0:T(8,128)(2,1)}, bf16[4096,256]{1,0:T(8,128)(2,1)}) custom-call(bf16[128,4096]{1,0:T(8,128)(2,1)S(1)} %get-tuple-element.96.refs_0_.refs_2_, bf16[128,256]{1,0:T(8,128)(2,1)S(1)} %get-tuple-element.97.refs_1_, bf16[128,4096]{1,0:T(8,128)(2,1)S(1)} %get-tuple-element.96.refs_0_.refs_2_, ...), custom_call_target="tpu_custom_call" | custom-call | tf_op jit(solution)/shard_map/pallas_call | solution.py:219
  74.9 1.2 %shard_map.121 = bf16[128,4096]{1,0:T(8,128)(2,1)} custom-call(bf16[16,128]{1,0:T(8,128)(2,1)S(1)} %get-tuple-element.54.refs_0_, bf16[4,4096]{1,0:T(4,128)(2,1)S(1)} %get-tuple-element.92.refs_1_, bf16[4,4096]{1,0:T(4,128)(2,1)S(1)} %collective-permute-done.37.refs_2_, bf16[4,4096]{1,0:T(4,128)(2,1)S(1)} %collective-permute-done.38.refs_3_, ...), custom_call_target="tpu_custom_call" | custom-call | tf_op jit(solution)/shard_map/pallas_call | solution.py:190
  76.2 1.3 %shard_map.117 = bf16[128,4096]{1,0:T(8,128)(2,1)} custom-call(bf16[16,128]{1,0:T(8,128)(2,1)S(1)} %get-tuple-element.54.refs_0_, f32[16,128]{1,0:T(8,128)S(1)} %get-tuple-element.55.refs_1_, bf16[4,4096]{1,0:T(4,128)(2,1)S(1)} %get-tuple-element.71.refs_2_, bf16[4,4096]{1,0:T(4,128)(2,1)S(1)} %collective-permute-done.17.refs_3_, ...), custom_call_target="tpu_custom_call" | custom-call | tf_op jit(solution)/shard_map/pallas_call | solution.py:190
  (56 shorter events, 3.0 us)
Async XLA Ops:
  2.5 5.3 %collective-permute-start = (bf16[4,4096]{1,0:T(4,128)(2,1)S(1)}, bf16[4,4096]{1,0:T(4,128)(2,1)S(1)}, u32[]{:S(2)}, u32[]{:S(2)}) collective-permute-start(bf16[4,4096]{1,0:T(4,128)(2,1)S(1)} %get-tuple-element.57), channel_id=1, source_target_pairs={{0,1},{1,0},{2,3},{3,2},{4,5},{5,4},{6,7},{7,6},{8,9},{9,8},{10,11... | collective-permute-start | bytes 98312 | tf_op jit(solution)/shard_map/ppermute | solution.py:364
  3.1 4.7 %collective-permute-start.1 = (bf16[4,4096]{1,0:T(4,128)(2,1)S(1)}, bf16[4,4096]{1,0:T(4,128)(2,1)S(1)}, u32[]{:S(2)}, u32[]{:S(2)}) collective-permute-start(bf16[4,4096]{1,0:T(4,128)(2,1)S(1)} %get-tuple-element.58), channel_id=1, source_target_pairs={{0,2},{1,3},{2,0},{3,1},{4,6},{5,7},{6,4},{7,5},{8,10},{9,11},{10,... | collective-permute-start | bytes 98312 | tf_op jit(solution)/shard_map/ppermute | solution.py:364
  5.7 3.4 %collective-permute-start.2 = (bf16[4,4096]{1,0:T(4,128)(2,1)S(1)}, bf16[4,4096]{1,0:T(4,128)(2,1)S(1)}, u32[]{:S(2)}, u32[]{:S(2)}) collective-permute-start(bf16[4,4096]{1,0:T(4,128)(2,1)S(1)} %get-tuple-element.59), channel_id=1, source_target_pairs={{0,3},{1,2},{2,1},{3,0},{4,7},{5,6},{6,5},{7,4},{8,11},{9,10},{10,... | collective-permute-start | bytes 98312 | tf_op jit(solution)/shard_map/ppermute | solution.py:364
  5.7 5.0 %collective-permute-start.20 = (bf16[4,4096]{1,0:T(4,128)(2,1)S(1)}, bf16[4,4096]{1,0:T(4,128)(2,1)S(1)}, u32[]{:S(2)}, u32[]{:S(2)}) collective-permute-start(bf16[4,4096]{1,0:T(4,128)(2,1)S(1)} %get-tuple-element.76), channel_id=1, source_target_pairs={{0,1},{1,0},{2,3},{3,2},{4,5},{5,4},{6,7},{7,6},{8,9},{9,8},{10,11... | collective-permute-start | bytes 98312 | tf_op jit(solution)/shard_map/ppermute | solution.py:364
  5.8 4.8 %collective-permute-start.21 = (bf16[4,4096]{1,0:T(4,128)(2,1)S(1)}, bf16[4,4096]{1,0:T(4,128)(2,1)S(1)}, u32[]{:S(2)}, u32[]{:S(2)}) collective-permute-start(bf16[4,4096]{1,0:T(4,128)(2,1)S(1)} %get-tuple-element.77), channel_id=1, source_target_pairs={{0,2},{1,3},{2,0},{3,1},{4,6},{5,7},{6,4},{7,5},{8,10},{9,11},{10,... | collective-permute-start | bytes 98312 | tf_op jit(solution)/shard_map/ppermute | solution.py:364
  7.8 3.6 %collective-permute-start.22 = (bf16[4,4096]{1,0:T(4,128)(2,1)S(1)}, bf16[4,4096]{1,0:T(4,128)(2,1)S(1)}, u32[]{:S(2)}, u32[]{:S(2)}) collective-permute-start(bf16[4,4096]{1,0:T(4,128)(2,1)S(1)} %get-tuple-element.78), channel_id=1, source_target_pairs={{0,3},{1,2},{2,1},{3,0},{4,7},{5,6},{6,5},{7,4},{8,11},{9,10},{10,... | collective-permute-start | bytes 98312 | tf_op jit(solution)/shard_map/ppermute | solution.py:364
  9.1 5.9 %collective-permute-start.6 = (bf16[16,4096]{1,0:T(8,128)(2,1)S(1)}, bf16[16,4096]{1,0:T(8,128)(2,1)S(1)}, u32[]{:S(2)}, u32[]{:S(2)}) collective-permute-start(bf16[16,4096]{1,0:T(8,128)(2,1)S(1)} %shard_map.111.refs_0_), channel_id=1, source_target_pairs={{0,8},{8,16},{16,24},{24,28},{28,20},{20,12},{12,4},{4,0},{1,9},{9... | collective-permute-start | bytes 393224 | tf_op jit(solution)/shard_map/ppermute | solution.py:317
  11.5 6.7 %collective-permute-start.23 = (bf16[16,4096]{1,0:T(8,128)(2,1)S(1)}, bf16[16,4096]{1,0:T(8,128)(2,1)S(1)}, u32[]{:S(2)}, u32[]{:S(2)}) collective-permute-start(bf16[16,4096]{1,0:T(8,128)(2,1)S(1)} %shard_map.118.refs_0_), channel_id=1, source_target_pairs={{0,4},{8,0},{16,8},{24,16},{28,24},{20,28},{12,20},{4,12},{1,5},{9... | collective-permute-start | bytes 393224 | tf_op jit(solution)/shard_map/ppermute | solution.py:317
  13.0 6.9 %collective-permute-start.3 = (bf16[16,4096]{1,0:T(8,128)(2,1)S(1)}, bf16[16,4096]{1,0:T(8,128)(2,1)S(1)}, u32[]{:S(2)}, u32[]{:S(2)}) collective-permute-start(bf16[16,4096]{1,0:T(8,128)(2,1)S(1)} %shard_map.111.refs_0_), channel_id=1, source_target_pairs={{0,4},{8,0},{16,8},{24,16},{28,24},{20,28},{12,20},{4,12},{1,5},{9... | collective-permute-start | bytes 393224 | tf_op jit(solution)/shard_map/ppermute | solution.py:317
  15.0 7.2 %collective-permute-start.7 = (bf16[16,4096]{1,0:T(8,128)(2,1)S(1)}, bf16[16,4096]{1,0:T(8,128)(2,1)S(1)}, u32[]{:S(2)}, u32[]{:S(2)}) collective-permute-start(bf16[16,4096]{1,0:T(8,128)(2,1)S(1)} %collective-permute-done.6.refs_7_), channel_id=1, source_target_pairs={{0,8},{8,16},{16,24},{24,28},{28,20},{20,12},{12,4},{4,0},{1,9},{9... | collective-permute-start | bytes 393224 | tf_op jit(solution)/shard_map/ppermute | solution.py:317
  16.6 6.4 %collective-permute-start.27 = (bf16[16,4096]{1,0:T(8,128)(2,1)S(1)}, bf16[16,4096]{1,0:T(8,128)(2,1)S(1)}, u32[]{:S(2)}, u32[]{:S(2)}) collective-permute-start(bf16[16,4096]{1,0:T(8,128)(2,1)S(1)} %shard_map.118.refs_0_), channel_id=1, source_target_pairs={{0,8},{8,16},{16,24},{24,28},{28,20},{20,12},{12,4},{4,0},{1,9},{9... | collective-permute-start | bytes 393224 | tf_op jit(solution)/shard_map/ppermute | solution.py:317
  18.1 7.2 %collective-permute-start.24 = (bf16[16,4096]{1,0:T(8,128)(2,1)S(1)}, bf16[16,4096]{1,0:T(8,128)(2,1)S(1)}, u32[]{:S(2)}, u32[]{:S(2)}) collective-permute-start(bf16[16,4096]{1,0:T(8,128)(2,1)S(1)} %collective-permute-done.23.refs_1_), channel_id=1, source_target_pairs={{0,4},{8,0},{16,8},{24,16},{28,24},{20,28},{12,20},{4,12},{1,5},{9... | collective-permute-start | bytes 393224 | tf_op jit(solution)/shard_map/ppermute | solution.py:317
  19.9 6.4 %collective-permute-start.4 = (bf16[16,4096]{1,0:T(8,128)(2,1)S(1)}, bf16[16,4096]{1,0:T(8,128)(2,1)S(1)}, u32[]{:S(2)}, u32[]{:S(2)}) collective-permute-start(bf16[16,4096]{1,0:T(8,128)(2,1)S(1)} %collective-permute-done.3.refs_1_), channel_id=1, source_target_pairs={{0,4},{8,0},{16,8},{24,16},{28,24},{20,28},{12,20},{4,12},{1,5},{9... | collective-permute-start | bytes 393224 | tf_op jit(solution)/shard_map/ppermute | solution.py:317
  22.2 6.2 %collective-permute-start.8 = (bf16[16,4096]{1,0:T(8,128)(2,1)S(1)}, bf16[16,4096]{1,0:T(8,128)(2,1)S(1)}, u32[]{:S(2)}, u32[]{:S(2)}) collective-permute-start(bf16[16,4096]{1,0:T(8,128)(2,1)S(1)} %collective-permute-done.7.refs_6_), channel_id=1, source_target_pairs={{0,8},{8,16},{16,24},{24,28},{28,20},{20,12},{12,4},{4,0},{1,9},{9... | collective-permute-start | bytes 393224 | tf_op jit(solution)/shard_map/ppermute | solution.py:317
  22.9 6.3 %collective-permute-start.28 = (bf16[16,4096]{1,0:T(8,128)(2,1)S(1)}, bf16[16,4096]{1,0:T(8,128)(2,1)S(1)}, u32[]{:S(2)}, u32[]{:S(2)}) collective-permute-start(bf16[16,4096]{1,0:T(8,128)(2,1)S(1)} %collective-permute-done.27.refs_7_), channel_id=1, source_target_pairs={{0,8},{8,16},{16,24},{24,28},{28,20},{20,12},{12,4},{4,0},{1,9},{9... | collective-permute-start | bytes 393224 | tf_op jit(solution)/shard_map/ppermute | solution.py:317
  25.3 6.3 %collective-permute-start.25 = (bf16[16,4096]{1,0:T(8,128)(2,1)S(1)}, bf16[16,4096]{1,0:T(8,128)(2,1)S(1)}, u32[]{:S(2)}, u32[]{:S(2)}) collective-permute-start(bf16[16,4096]{1,0:T(8,128)(2,1)S(1)} %collective-permute-done.24.refs_2_), channel_id=1, source_target_pairs={{0,4},{8,0},{16,8},{24,16},{28,24},{20,28},{12,20},{4,12},{1,5},{9... | collective-permute-start | bytes 393224 | tf_op jit(solution)/shard_map/ppermute | solution.py:317
  26.4 12.0 %collective-permute-start.5 = (bf16[16,4096]{1,0:T(8,128)(2,1)S(1)}, bf16[16,4096]{1,0:T(8,128)(2,1)S(1)}, u32[]{:S(2)}, u32[]{:S(2)}) collective-permute-start(bf16[16,4096]{1,0:T(8,128)(2,1)S(1)} %collective-permute-done.4.refs_2_), channel_id=1, source_target_pairs={{0,4},{8,0},{16,8},{24,16},{28,24},{20,28},{12,20},{4,12},{1,5},{9... | collective-permute-start | bytes 393224 | tf_op jit(solution)/shard_map/ppermute | solution.py:317
  28.4 9.9 %collective-permute-start.9 = (bf16[16,4096]{1,0:T(8,128)(2,1)S(1)}, bf16[16,4096]{1,0:T(8,128)(2,1)S(1)}, u32[]{:S(2)}, u32[]{:S(2)}) collective-permute-start(bf16[16,4096]{1,0:T(8,128)(2,1)S(1)} %collective-permute-done.8.refs_5_), channel_id=1, source_target_pairs={{0,8},{8,16},{16,24},{24,28},{28,20},{20,12},{12,4},{4,0},{1,9},{9... | collective-permute-start | bytes 393224 | tf_op jit(solution)/shard_map/ppermute | solution.py:317
  29.2 10.3 %collective-permute-start.29 = (bf16[16,4096]{1,0:T(8,128)(2,1)S(1)}, bf16[16,4096]{1,0:T(8,128)(2,1)S(1)}, u32[]{:S(2)}, u32[]{:S(2)}) collective-permute-start(bf16[16,4096]{1,0:T(8,128)(2,1)S(1)} %collective-permute-done.28.refs_6_), channel_id=1, source_target_pairs={{0,8},{8,16},{16,24},{24,28},{28,20},{20,12},{12,4},{4,0},{1,9},{9... | collective-permute-start | bytes 393224 | tf_op jit(solution)/shard_map/ppermute | solution.py:317
  31.6 7.9 %collective-permute-start.26 = (bf16[16,4096]{1,0:T(8,128)(2,1)S(1)}, bf16[16,4096]{1,0:T(8,128)(2,1)S(1)}, u32[]{:S(2)}, u32[]{:S(2)}) collective-permute-start(bf16[16,4096]{1,0:T(8,128)(2,1)S(1)} %collective-permute-done.25.refs_3_), channel_id=1, source_target_pairs={{0,4},{8,0},{16,8},{24,16},{28,24},{20,28},{12,20},{4,12},{1,5},{9... | collective-permute-start | bytes 393224 | tf_op jit(solution)/shard_map/ppermute | solution.py:317
  41.1 6.4 %collective-permute-start.34 = (bf16[16,4096]{1,0:T(8,128)(2,1)S(1)}, bf16[16,4096]{1,0:T(8,128)(2,1)S(1)}, u32[]{:S(2)}, u32[]{:S(2)}) collective-permute-start(bf16[16,4096]{1,0:T(8,128)(2,1)S(1)} %get-tuple-element.89), channel_id=1, source_target_pairs={{0,8},{8,16},{16,24},{24,28},{28,20},{20,12},{12,4},{4,0},{1,9},{9... | collective-permute-start | bytes 393224 | tf_op jit(solution)/shard_map/ppermute | solution.py:317
  43.2 6.4 %collective-permute-start.30 = (bf16[16,4096]{1,0:T(8,128)(2,1)S(1)}, bf16[16,4096]{1,0:T(8,128)(2,1)S(1)}, u32[]{:S(2)}, u32[]{:S(2)}) collective-permute-start(bf16[16,4096]{1,0:T(8,128)(2,1)S(1)} %get-tuple-element.85), channel_id=1, source_target_pairs={{0,4},{8,0},{16,8},{24,16},{28,24},{20,28},{12,20},{4,12},{1,5},{9... | collective-permute-start | bytes 393224 | tf_op jit(solution)/shard_map/ppermute | solution.py:317
  43.2 8.3 %collective-permute-start.14 = (bf16[16,4096]{1,0:T(8,128)(2,1)S(1)}, bf16[16,4096]{1,0:T(8,128)(2,1)S(1)}, u32[]{:S(2)}, u32[]{:S(2)}) collective-permute-start(bf16[16,4096]{1,0:T(8,128)(2,1)S(1)} %get-tuple-element.68), channel_id=1, source_target_pairs={{0,4},{8,0},{16,8},{24,16},{28,24},{20,28},{12,20},{4,12},{1,5},{9... | collective-permute-start | bytes 393224 | tf_op jit(solution)/shard_map/ppermute | solution.py:317
  44.7 7.3 %collective-permute-start.10 = (bf16[16,4096]{1,0:T(8,128)(2,1)S(1)}, bf16[16,4096]{1,0:T(8,128)(2,1)S(1)}, u32[]{:S(2)}, u32[]{:S(2)}) collective-permute-start(bf16[16,4096]{1,0:T(8,128)(2,1)S(1)} %get-tuple-element.64), channel_id=1, source_target_pairs={{0,8},{8,16},{16,24},{24,28},{28,20},{20,12},{12,4},{4,0},{1,9},{9... | collective-permute-start | bytes 393224 | tf_op jit(solution)/shard_map/ppermute | solution.py:317
  47.6 6.4 %collective-permute-start.35 = (bf16[16,4096]{1,0:T(8,128)(2,1)S(1)}, bf16[16,4096]{1,0:T(8,128)(2,1)S(1)}, u32[]{:S(2)}, u32[]{:S(2)}) collective-permute-start(bf16[16,4096]{1,0:T(8,128)(2,1)S(1)} %add_convert_fusion.1), channel_id=1, source_target_pairs={{0,8},{8,16},{16,24},{24,28},{28,20},{20,12},{12,4},{4,0},{1,9},{9... | collective-permute-start | bytes 393224 | tf_op jit(solution)/shard_map/ppermute | solution.py:317
  49.6 6.5 %collective-permute-start.31 = (bf16[16,4096]{1,0:T(8,128)(2,1)S(1)}, bf16[16,4096]{1,0:T(8,128)(2,1)S(1)}, u32[]{:S(2)}, u32[]{:S(2)}) collective-permute-start(bf16[16,4096]{1,0:T(8,128)(2,1)S(1)} %add_convert_fusion.4), channel_id=1, source_target_pairs={{0,4},{8,0},{16,8},{24,16},{28,24},{20,28},{12,20},{4,12},{1,5},{9... | collective-permute-start | bytes 393224 | tf_op jit(solution)/shard_map/ppermute | solution.py:317
  51.6 6.4 %collective-permute-start.15 = (bf16[16,4096]{1,0:T(8,128)(2,1)S(1)}, bf16[16,4096]{1,0:T(8,128)(2,1)S(1)}, u32[]{:S(2)}, u32[]{:S(2)}) collective-permute-start(bf16[16,4096]{1,0:T(8,128)(2,1)S(1)} %add_convert_fusion.6), channel_id=1, source_target_pairs={{0,4},{8,0},{16,8},{24,16},{28,24},{20,28},{12,20},{4,12},{1,5},{9... | collective-permute-start | bytes 393224 | tf_op jit(solution)/shard_map/ppermute | solution.py:317
  52.0 6.5 %collective-permute-start.11 = (bf16[16,4096]{1,0:T(8,128)(2,1)S(1)}, bf16[16,4096]{1,0:T(8,128)(2,1)S(1)}, u32[]{:S(2)}, u32[]{:S(2)}) collective-permute-start(bf16[16,4096]{1,0:T(8,128)(2,1)S(1)} %add_convert_fusion.9), channel_id=1, source_target_pairs={{0,8},{8,16},{16,24},{24,28},{28,20},{20,12},{12,4},{4,0},{1,9},{9... | collective-permute-start | bytes 393224 | tf_op jit(solution)/shard_map/ppermute | solution.py:317
  54.0 11.2 %collective-permute-start.36 = (bf16[16,4096]{1,0:T(8,128)(2,1)S(1)}, bf16[16,4096]{1,0:T(8,128)(2,1)S(1)}, u32[]{:S(2)}, u32[]{:S(2)}) collective-permute-start(bf16[16,4096]{1,0:T(8,128)(2,1)S(1)} %add_convert_fusion), channel_id=1, source_target_pairs={{0,8},{8,16},{16,24},{24,28},{28,20},{20,12},{12,4},{4,0},{1,9},{9... | collective-permute-start | bytes 393224 | tf_op jit(solution)/shard_map/ppermute | solution.py:317
  56.1 5.0 %collective-permute-start.32 = (bf16[16,4096]{1,0:T(8,128)(2,1)S(1)}, bf16[16,4096]{1,0:T(8,128)(2,1)S(1)}, u32[]{:S(2)}, u32[]{:S(2)}) collective-permute-start(bf16[16,4096]{1,0:T(8,128)(2,1)S(1)} %add_convert_fusion.3), channel_id=1, source_target_pairs={{0,4},{8,0},{16,8},{24,16},{28,24},{20,28},{12,20},{4,12},{1,5},{9... | collective-permute-start | bytes 393224 | tf_op jit(solution)/shard_map/ppermute | solution.py:317
  58.0 10.1 %collective-permute-start.16 = (bf16[16,4096]{1,0:T(8,128)(2,1)S(1)}, bf16[16,4096]{1,0:T(8,128)(2,1)S(1)}, u32[]{:S(2)}, u32[]{:S(2)}) collective-permute-start(bf16[16,4096]{1,0:T(8,128)(2,1)S(1)} %add_convert_fusion.5), channel_id=1, source_target_pairs={{0,4},{8,0},{16,8},{24,16},{28,24},{20,28},{12,20},{4,12},{1,5},{9... | collective-permute-start | bytes 393224 | tf_op jit(solution)/shard_map/ppermute | solution.py:317
  58.6 5.0 %collective-permute-start.12 = (bf16[16,4096]{1,0:T(8,128)(2,1)S(1)}, bf16[16,4096]{1,0:T(8,128)(2,1)S(1)}, u32[]{:S(2)}, u32[]{:S(2)}) collective-permute-start(bf16[16,4096]{1,0:T(8,128)(2,1)S(1)} %add_convert_fusion.8), channel_id=1, source_target_pairs={{0,8},{8,16},{16,24},{24,28},{28,20},{20,12},{12,4},{4,0},{1,9},{9... | collective-permute-start | bytes 393224 | tf_op jit(solution)/shard_map/ppermute | solution.py:317
  61.2 5.0 %collective-permute-start.33 = (bf16[16,4096]{1,0:T(8,128)(2,1)S(1)}, bf16[16,4096]{1,0:T(8,128)(2,1)S(1)}, u32[]{:S(2)}, u32[]{:S(2)}) collective-permute-start(bf16[16,4096]{1,0:T(8,128)(2,1)S(1)} %add_convert_fusion.2), channel_id=1, source_target_pairs={{0,4},{8,0},{16,8},{24,16},{28,24},{20,28},{12,20},{4,12},{1,5},{9... | collective-permute-start | bytes 393224 | tf_op jit(solution)/shard_map/ppermute | solution.py:317
  63.7 5.0 %collective-permute-start.13 = (bf16[16,4096]{1,0:T(8,128)(2,1)S(1)}, bf16[16,4096]{1,0:T(8,128)(2,1)S(1)}, u32[]{:S(2)}, u32[]{:S(2)}) collective-permute-start(bf16[16,4096]{1,0:T(8,128)(2,1)S(1)} %add_convert_fusion.7), channel_id=1, source_target_pairs={{0,8},{8,16},{16,24},{24,28},{28,20},{20,12},{12,4},{4,0},{1,9},{9... | collective-permute-start | bytes 393224 | tf_op jit(solution)/shard_map/ppermute | solution.py:317
  66.2 3.1 %collective-permute-start.37 = (bf16[4,4096]{1,0:T(4,128)(2,1)S(1)}, bf16[4,4096]{1,0:T(4,128)(2,1)S(1)}, u32[]{:S(2)}, u32[]{:S(2)}) collective-permute-start(bf16[4,4096]{1,0:T(4,128)(2,1)S(1)} %get-tuple-element.93), channel_id=1, source_target_pairs={{0,1},{1,0},{2,3},{3,2},{4,5},{5,4},{6,7},{7,6},{8,9},{9,8},{10,11... | collective-permute-start | bytes 98312 | tf_op jit(solution)/shard_map/ppermute | solution.py:364
  66.3 8.6 %collective-permute-start.38 = (bf16[4,4096]{1,0:T(4,128)(2,1)S(1)}, bf16[4,4096]{1,0:T(4,128)(2,1)S(1)}, u32[]{:S(2)}, u32[]{:S(2)}) collective-permute-start(bf16[4,4096]{1,0:T(4,128)(2,1)S(1)} %get-tuple-element.94), channel_id=1, source_target_pairs={{0,2},{1,3},{2,0},{3,1},{4,6},{5,7},{6,4},{7,5},{8,10},{9,11},{10,... | collective-permute-start | bytes 98312 | tf_op jit(solution)/shard_map/ppermute | solution.py:364
  66.4 8.5 %collective-permute-start.39 = (bf16[4,4096]{1,0:T(4,128)(2,1)S(1)}, bf16[4,4096]{1,0:T(4,128)(2,1)S(1)}, u32[]{:S(2)}, u32[]{:S(2)}) collective-permute-start(bf16[4,4096]{1,0:T(4,128)(2,1)S(1)} %get-tuple-element.95), channel_id=1, source_target_pairs={{0,3},{1,2},{2,1},{3,0},{4,7},{5,6},{6,5},{7,4},{8,11},{9,10},{10,... | collective-permute-start | bytes 98312 | tf_op jit(solution)/shard_map/ppermute | solution.py:364
  68.7 7.4 %collective-permute-start.17 = (bf16[4,4096]{1,0:T(4,128)(2,1)S(1)}, bf16[4,4096]{1,0:T(4,128)(2,1)S(1)}, u32[]{:S(2)}, u32[]{:S(2)}) collective-permute-start(bf16[4,4096]{1,0:T(4,128)(2,1)S(1)} %get-tuple-element.72), channel_id=1, source_target_pairs={{0,1},{1,0},{2,3},{3,2},{4,5},{5,4},{6,7},{7,6},{8,9},{9,8},{10,11... | collective-permute-start | bytes 98312 | tf_op jit(solution)/shard_map/ppermute | solution.py:364
  68.8 7.4 %collective-permute-start.18 = (bf16[4,4096]{1,0:T(4,128)(2,1)S(1)}, bf16[4,4096]{1,0:T(4,128)(2,1)S(1)}, u32[]{:S(2)}, u32[]{:S(2)}) collective-permute-start(bf16[4,4096]{1,0:T(4,128)(2,1)S(1)} %get-tuple-element.73), channel_id=1, source_target_pairs={{0,2},{1,3},{2,0},{3,1},{4,6},{5,7},{6,4},{7,5},{8,10},{9,11},{10,... | collective-permute-start | bytes 98312 | tf_op jit(solution)/shard_map/ppermute | solution.py:364
  69.4 6.8 %collective-permute-start.19 = (bf16[4,4096]{1,0:T(4,128)(2,1)S(1)}, bf16[4,4096]{1,0:T(4,128)(2,1)S(1)}, u32[]{:S(2)}, u32[]{:S(2)}) collective-permute-start(bf16[4,4096]{1,0:T(4,128)(2,1)S(1)} %get-tuple-element.74), channel_id=1, source_target_pairs={{0,3},{1,2},{2,1},{3,0},{4,7},{5,6},{6,5},{7,4},{8,11},{9,10},{10,... | collective-permute-start | bytes 98312 | tf_op jit(solution)/shard_map/ppermute | solution.py:364

commit v2 on v1

--- a/solution.py
+++ b/solution.py
@@ -53,12 +53,12 @@
     return [pltpu.with_memory_space_constraint(v, pltpu.HBM) for v in arrays]
 
 
-def pack(rank_id, ids, weights, tokens, cotangent, n_rep):
+def pack(ids, weights, tokens, cotangent, n_rep):
     tok, width = tokens.shape
     slots = n_rep * CAP
     given = [ids, weights, tokens, cotangent]
 
-    def body(rank_ref, *refs):
+    def body(*refs):
         ins, outs = refs[:4], refs[4 : 4 + 2 * n_rep]
         pick_ref, scale_ref = refs[4 + 2 * n_rep : 6 + 2 * n_rep]
         held, sems = refs[6 + 2 * n_rep : 10 + 2 * n_rep], refs[-1]
@@ -70,7 +70,7 @@
             copy.start()
         copies[0].wait()
         copies[1].wait()
-        chosen, first = selection(rank_ref[0], held[0][...], n_rep)
+        chosen, first = selection(lax.axis_index("rep"), held[0][...], n_rep)
         scale = slot_weights(chosen, first, held[1][...])
         pick = jnp.where(chosen, 1.0, 0.0).astype(BF)
         pick_ref[...] = pick
@@ -88,33 +88,20 @@
         body,
         out_shape=[jax.ShapeDtypeStruct((CAP, width), BF)] * (2 * n_rep)
         + [jax.ShapeDtypeStruct((slots, tok), BF), jax.ShapeDtypeStruct((slots, tok), F32)],
-        in_specs=[SMEM] + [HBM] * 4,
+        in_specs=[HBM] * 4,
         out_specs=[VMEM] * (2 * n_rep + 2),
         scratch_shapes=[pltpu.VMEM(v.shape, v.dtype) for v in given]
         + [pltpu.SemaphoreType.DMA((4,))],
         compiler_params=pltpu.CompilerParams(vmem_limit_bytes=12 << 20),
-    )(rank_id, *in_hbm(given))
+    )(*in_hbm(given))
     return out[:n_rep], out[n_rep : 2 * n_rep], out[-2], out[-1]
 
 
-def load(array):
-    def body(src, dst, turned, sem):
-        copy = pltpu.make_async_copy(src, dst, sem)
-        copy.start()
-        copy.wait()
-        turned[...] = dst[...].T
-
-    return pl.pallas_call(
-        body,
-        out_shape=[
-            jax.ShapeDtypeStruct(array.shape, array.dtype),
-            jax.ShapeDtypeStruct(array.shape[::-1], array.dtype),
-        ],
-        in_specs=[HBM],
-        out_specs=[VMEM] * 2,
-        scratch_shapes=[pltpu.SemaphoreType.DMA],
-        compiler_params=pltpu.CompilerParams(vmem_limit_bytes=12 << 20),
-    )(*in_hbm([array]))
+def turn(array):
+    def body(src, dst):
+        dst[...] = src[...].T
+
+    return call(body, jax.ShapeDtypeStruct(array.shape[::-1], array.dtype), 1)(array)
 
 
 def join(blocks):
@@ -194,7 +181,7 @@
     count = len(jobs)
     shapes = [(left.shape[1], right.shape[1]) for left, right in jobs]
     flat = [v for job in jobs for v in job]
-    tiles = 4
+    tiles = 8
 
     def body(*refs):
         ins, outs = refs[: 2 * count], refs[2 * count : 3 * count]
@@ -367,17 +354,14 @@
 
 def local(tokens, expert_ids, route_weights, w_gate, w_up, w_down, cotangent):
     n_rep = lax.axis_size("rep")
-    rank_id = lax.axis_index("rep").astype(jnp.int32).reshape(1)
     ids = expert_ids.T
     weights = route_weights.T
 
-    sent, sent_ups, pick, scale = pack(rank_id, ids, weights, tokens, cotangent, n_rep)
+    sent, sent_ups, pick, scale = pack(ids, weights, tokens, cotangent, n_rep)
     token_rows = join(trade(sent))
     up_rows = join(trade(sent_ups))
-    wg, wg_turned = load(w_gate[0])
-    wu, wu_turned = load(w_up[0])
-    wd, wd_turned = load(w_down[0])
-    plain, turned = (wg, wu, wd), (wg_turned, wu_turned, wd_turned)
+    plain = [w_gate[0], w_up[0], w_down[0]]
+    turned = [turn(w) for w in plain]
     token_chunks = ring_gather(token_rows, 1)
     up_chunks = ring_gather(up_rows, -1)
     all_tokens, hidden, activated, slope, routed_parts = forward(token_chunks, *plain, 1)

time: 77.7 us -> 81 us (1.042)
  waiting for transfers between devices: 16.1 us -> 25.1 us
  Pallas kernels: 18.2 us -> 13.4 us
  starting transfers between devices: 42 us -> 37.8 us
  local copies, waits for them, and re-layouts: 0 us -> 3.18 us
    ppermute x28, waiting for transfers between devices: 14.2 us -> 19.4 us  [shift(): return lax.ppermute(value, ('ep', 'rep'), pairs)]
    pallas_call x3, Pallas kernels: 6.67 us -> 1.85 us  [turn(): call(body, jax.ShapeDtypeStruct(array.shape[::-1], array.dtype), 1)(array)]
    ppermute x28, starting transfers between devices: 32.8 us -> 28.9 us  [shift(): return lax.ppermute(value, ('ep', 'rep'), pairs)]
    ppermute x12, waiting for transfers between devices: 1.97 us -> 5.76 us  [trade(): found.append(lax.ppermute(blocks[k], 'rep', [(i, i ^ k) for i in range(n)]))]
    unnamed x0 -> x6, local copies, waits for them, and re-layouts: none -> 3.18 us
  transfers between devices with their start and end apart: 40 -> 40, of which waited for: 14 -> 14; matrix products, arithmetic and copies ran while one was open for 0% -> 0% of each run, Pallas kernels for 17% -> 12%
where the time goes in v2:
time: 81 us; the launch traced here: 80.7 us
  starting transfers between devices  37.8 us (47%)
  waiting for transfers between devices  25.1 us (31%)
  Pallas kernels  13.4 us (17%)
  local copies, waits for them, and re-layouts  3.18 us (4%)
  between operations  0.85 us (1%)
    ppermute x28, starting transfers between devices, shift(): return lax.ppermute(value, ('ep', 'rep'), pairs)  28.9 us
    ppermute x28, waiting for transfers between devices, shift(): return lax.ppermute(value, ('ep', 'rep'), pairs)  19.4 us
    ppermute x12, starting transfers between devices, trade(): found.append(lax.ppermute(blocks[k], 'rep', [(i, i ^ k) for i in range(n)]))  8.88 us
    ppermute x12, waiting for transfers between devices, trade(): found.append(lax.ppermute(blocks[k], 'rep', [(i, i ^ k) for i in range(n)]))  5.76 us
    pallas_call x2, Pallas kernels, weight_grads(): pl.pallas_call(body, out_shape=[jax.ShapeDtypeStruct(shape, BF) for shape...  4.09 us
    unnamed x6, local copies, waits for them, and re-layouts  3.18 us
    pallas_call x2, Pallas kernels, unpack(): return kernel(*lead, *blocks)[0]  2.53 us
    pallas_call x1, Pallas kernels, pack(): pl.pallas_call(body, out_shape=[jax.ShapeDtypeStruct((CAP, width), BF)] *...  2.02 us
  transfers between devices with their start and end apart: 40, of which 14 were waited for; matrix products, arithmetic and copies ran while one was open for 0% of the time, Pallas kernels for 12%

profile of v2, /device:TPU:0, one launch (start us, length us, event | category | flops | bytes accessed | tf_op | source)
XLA Modules:
  0.0 80.7 jit_solution(13406309975892100446)
XLA Ops:
  0.6 2.0 %shard_map.110 = (bf16[4,4096]{1,0:T(4,128)(2,1)S(1)}, bf16[4,4096]{1,0:T(4,128)(2,1)S(1)}, bf16[4,4096]{1,0:T(4,128)(2,1)S(1)}, bf16[4,4096]{1,0:T(4,128)(2,1)S...) custom-call(s32[2,128]{1,0:T(2,128)} %bitcast.15, ...), custom_call_target="tpu_custom_call" | custom-call | tf_op jit(solution)/shard_map/pallas_call | solution.py:87
  3.2 2.6 %collective-permute-start.1 = (bf16[4,4096]{1,0:T(4,128)(2,1)S(1)}, bf16[4,4096]{1,0:T(4,128)(2,1)S(1)}, u32[]{:S(2)}, u32[]{:S(2)}) collective-permute-start(bf16[4,4096]{1,0:T(4,128)(2,1)S(1)} %get-tuple-element.52), channel_id=1, source_target_pairs={{0,2},{1,3},{2,0},{3,1},{4,6},{5,7},{6,4},{7,5},{8,10},{9,11},{10,... | collective-permute-start | bytes 98312 | tf_op jit(solution)/shard_map/ppermute | solution.py:351
  5.8 1.9 %collective-permute-done.1.refs_2_ = bf16[4,4096]{1,0:T(4,128)(2,1)S(1)} collective-permute-done((bf16[4,4096]{1,0:T(4,128)(2,1)S(1)}, bf16[4,4096]{1,0:T(4,128)(2,1)S(1)}, u32[]{:S(2)}, u32[]{:S(2)}) %collective-permute-start.1) | collective-permute-done | bytes 32800 | tf_op jit(solution)/shard_map/ppermute | solution.py:351
  7.8 1.4 %collective-permute-done.2.refs_3_ = bf16[4,4096]{1,0:T(4,128)(2,1)S(1)} collective-permute-done((bf16[4,4096]{1,0:T(4,128)(2,1)S(1)}, bf16[4,4096]{1,0:T(4,128)(2,1)S(1)}, u32[]{:S(2)}, u32[]{:S(2)}) %collective-permute-start.2) | collective-permute-done | bytes 32800 | tf_op jit(solution)/shard_map/ppermute | solution.py:351
  9.2 1.6 %collective-permute-start.6 = (bf16[16,4096]{1,0:T(8,128)(2,1)S(1)}, bf16[16,4096]{1,0:T(8,128)(2,1)S(1)}, u32[]{:S(2)}, u32[]{:S(2)}) collective-permute-start(bf16[16,4096]{1,0:T(8,128)(2,1)S(1)} %shard_map.111.refs_0_), channel_id=1, source_target_pairs={{0,8},{8,16},{16,24},{24,28},{28,20},{20,12},{12,4},{4,0},{1,9},{9... | collective-permute-start | bytes 393224 | tf_op jit(solution)/shard_map/ppermute | solution.py:304
  10.8 0.8 %collective-permute-start.21 = (bf16[4,4096]{1,0:T(4,128)(2,1)S(1)}, bf16[4,4096]{1,0:T(4,128)(2,1)S(1)}, u32[]{:S(2)}, u32[]{:S(2)}) collective-permute-start(bf16[4,4096]{1,0:T(4,128)(2,1)S(1)} %get-tuple-element.68), channel_id=1, source_target_pairs={{0,2},{1,3},{2,0},{3,1},{4,6},{5,7},{6,4},{7,5},{8,10},{9,11},{10,... | collective-permute-start | bytes 98312 | tf_op jit(solution)/shard_map/ppermute | solution.py:351
  11.7 1.0 %collective-permute-start.22 = (bf16[4,4096]{1,0:T(4,128)(2,1)S(1)}, bf16[4,4096]{1,0:T(4,128)(2,1)S(1)}, u32[]{:S(2)}, u32[]{:S(2)}) collective-permute-start(bf16[4,4096]{1,0:T(4,128)(2,1)S(1)} %get-tuple-element.69), channel_id=1, source_target_pairs={{0,3},{1,2},{2,1},{3,0},{4,7},{5,6},{6,5},{7,4},{8,11},{9,10},{10,... | collective-permute-start | bytes 98312 | tf_op jit(solution)/shard_map/ppermute | solution.py:351
  12.7 2.1 %collective-permute-done.21.refs_2_ = bf16[4,4096]{1,0:T(4,128)(2,1)S(1)} collective-permute-done((bf16[4,4096]{1,0:T(4,128)(2,1)S(1)}, bf16[4,4096]{1,0:T(4,128)(2,1)S(1)}, u32[]{:S(2)}, u32[]{:S(2)}) %collective-permute-start.21) | collective-permute-done | bytes 32800 | tf_op jit(solution)/shard_map/ppermute | solution.py:351
  15.2 0.6 collective-permute-start.23
  15.8 1.4 %collective-permute-start.3 = (bf16[16,4096]{1,0:T(8,128)(2,1)S(1)}, bf16[16,4096]{1,0:T(8,128)(2,1)S(1)}, u32[]{:S(2)}, u32[]{:S(2)}) collective-permute-start(bf16[16,4096]{1,0:T(8,128)(2,1)S(1)} %shard_map.111.refs_0_), channel_id=1, source_target_pairs={{0,4},{8,0},{16,8},{24,16},{28,24},{20,28},{12,20},{4,12},{1,5},{9... | collective-permute-start | bytes 393224 | tf_op jit(solution)/shard_map/ppermute | solution.py:304
  17.2 0.7 collective-permute-start.7
  17.8 1.5 %collective-permute-start.27 = (bf16[16,4096]{1,0:T(8,128)(2,1)S(1)}, bf16[16,4096]{1,0:T(8,128)(2,1)S(1)}, u32[]{:S(2)}, u32[]{:S(2)}) collective-permute-start(bf16[16,4096]{1,0:T(8,128)(2,1)S(1)} %shard_map.115.refs_0_), channel_id=1, source_target_pairs={{0,8},{8,16},{16,24},{24,28},{28,20},{20,12},{12,4},{4,0},{1,9},{9... | collective-permute-start | bytes 393224 | tf_op jit(solution)/shard_map/ppermute | solution.py:304
  19.3 2.3 %collective-permute-done.23.refs_1_ = bf16[16,4096]{1,0:T(8,128)(2,1)S(1)} collective-permute-done((bf16[16,4096]{1,0:T(8,128)(2,1)S(1)}, bf16[16,4096]{1,0:T(8,128)(2,1)S(1)}, u32[]{:S(2)}, u32[]{:S(2)}) %collective-permute-start.23) | collective-permute-done | bytes 131104 | tf_op jit(solution)/shard_map/ppermute | solution.py:304
  22.2 2.2 %collective-permute-done.3.refs_1_ = bf16[16,4096]{1,0:T(8,128)(2,1)S(1)} collective-permute-done((bf16[16,4096]{1,0:T(8,128)(2,1)S(1)}, bf16[16,4096]{1,0:T(8,128)(2,1)S(1)}, u32[]{:S(2)}, u32[]{:S(2)}) %collective-permute-start.3) | collective-permute-done | bytes 131104 | tf_op jit(solution)/shard_map/ppermute | solution.py:304
  25.0 1.5 %collective-permute-start.8 = (bf16[16,4096]{1,0:T(8,128)(2,1)S(1)}, bf16[16,4096]{1,0:T(8,128)(2,1)S(1)}, u32[]{:S(2)}, u32[]{:S(2)}) collective-permute-start(bf16[16,4096]{1,0:T(8,128)(2,1)S(1)} %collective-permute-done.7.refs_6_), channel_id=1, source_target_pairs={{0,8},{8,16},{16,24},{24,28},{28,20},{20,12},{12,4},{4,0},{1,9},{9... | collective-permute-start | bytes 393224 | tf_op jit(solution)/shard_map/ppermute | solution.py:304
  26.4 1.6 %collective-permute-start.28 = (bf16[16,4096]{1,0:T(8,128)(2,1)S(1)}, bf16[16,4096]{1,0:T(8,128)(2,1)S(1)}, u32[]{:S(2)}, u32[]{:S(2)}) collective-permute-start(bf16[16,4096]{1,0:T(8,128)(2,1)S(1)} %collective-permute-done.27.refs_7_), channel_id=1, source_target_pairs={{0,8},{8,16},{16,24},{24,28},{28,20},{20,12},{12,4},{4,0},{1,9},{9... | collective-permute-start | bytes 393224 | tf_op jit(solution)/shard_map/ppermute | solution.py:304
  28.5 2.0 %collective-permute-done.4.refs_2_ = bf16[16,4096]{1,0:T(8,128)(2,1)S(1)} collective-permute-done((bf16[16,4096]{1,0:T(8,128)(2,1)S(1)}, bf16[16,4096]{1,0:T(8,128)(2,1)S(1)}, u32[]{:S(2)}, u32[]{:S(2)}) %collective-permute-start.4) | collective-permute-done | bytes 131104 | tf_op jit(solution)/shard_map/ppermute | solution.py:304
  30.5 0.7 collective-permute-start.5
  31.2 1.3 %collective-permute-start.9 = (bf16[16,4096]{1,0:T(8,128)(2,1)S(1)}, bf16[16,4096]{1,0:T(8,128)(2,1)S(1)}, u32[]{:S(2)}, u32[]{:S(2)}) collective-permute-start(bf16[16,4096]{1,0:T(8,128)(2,1)S(1)} %collective-permute-done.8.refs_5_), channel_id=1, source_target_pairs={{0,8},{8,16},{16,24},{24,28},{28,20},{20,12},{12,4},{4,0},{1,9},{9... | collective-permute-start | bytes 393224 | tf_op jit(solution)/shard_map/ppermute | solution.py:304
  32.5 1.6 %collective-permute-start.29 = (bf16[16,4096]{1,0:T(8,128)(2,1)S(1)}, bf16[16,4096]{1,0:T(8,128)(2,1)S(1)}, u32[]{:S(2)}, u32[]{:S(2)}) collective-permute-start(bf16[16,4096]{1,0:T(8,128)(2,1)S(1)} %collective-permute-done.28.refs_6_), channel_id=1, source_target_pairs={{0,8},{8,16},{16,24},{24,28},{28,20},{20,12},{12,4},{4,0},{1,9},{9... | collective-permute-start | bytes 393224 | tf_op jit(solution)/shard_map/ppermute | solution.py:304
  34.6 1.8 %collective-permute-done.5.refs_3_ = bf16[16,4096]{1,0:T(8,128)(2,1)S(1)} collective-permute-done((bf16[16,4096]{1,0:T(8,128)(2,1)S(1)}, bf16[16,4096]{1,0:T(8,128)(2,1)S(1)}, u32[]{:S(2)}, u32[]{:S(2)}) %collective-permute-start.5) | collective-permute-done | bytes 131104 | tf_op jit(solution)/shard_map/ppermute | solution.py:304
  36.4 1.6 %copy-done.1 = bf16[1,4096,256]{2,1,0:T(8,128)(2,1)S(1)} copy-done((bf16[1,4096,256]{2,1,0:T(8,128)(2,1)S(1)}, bf16[1,4096,256]{2,1,0:T(8,128)(2,1)}, u32[]{:S(2)}) %copy-start.1) | copy-done | bytes 2097176
  38.0 1.6 %copy-done.2 = bf16[1,256,4096]{2,1,0:T(8,128)(2,1)S(1)} copy-done((bf16[1,256,4096]{2,1,0:T(8,128)(2,1)S(1)}, bf16[1,256,4096]{2,1,0:T(8,128)(2,1)}, u32[]{:S(2)}) %copy-start.2) | copy-done | bytes 2097176
  39.6 1.1 %shard_map.112 = (bf16[128,4096]{1,0:T(8,128)(2,1)S(1)}, bf16[128,256]{1,0:T(8,128)(2,1)S(1)}, f32[128,256]{1,0:T(8,128)S(1)}, f32[128,256]{1,0:T(8,128)S(1)}, f...) custom-call(bf16[16,4096]{1,0:T(8,128)(2,1)S(1)} %shard_map.111.refs, ...), custom_call_target="tpu_custom_call" | custom-call | tf_op jit(solution)/shard_map/pallas_call | solution.py:256
  40.7 1.6 %collective-permute-start.10 = (bf16[16,4096]{1,0:T(8,128)(2,1)S(1)}, bf16[16,4096]{1,0:T(8,128)(2,1)S(1)}, u32[]{:S(2)}, u32[]{:S(2)}) collective-permute-start(bf16[16,4096]{1,0:T(8,128)(2,1)S(1)} %get-tuple-element.55), channel_id=1, source_target_pairs={{0,8},{8,16},{16,24},{24,28},{28,20},{20,12},{12,4},{4,0},{1,9},{9... | collective-permute-start | bytes 393224 | tf_op jit(solution)/shard_map/ppermute | solution.py:304
  42.3 0.6 shard_map.116.refs_10_
  43.0 0.6 shard_map.117.refs_11_
  44.7 1.6 %shard_map.119 = (bf16[128,4096]{1,0:T(8,128)(2,1)S(1)}, bf16[128,256]{1,0:T(8,128)(2,1)S(1)}, bf16[128,256]{1,0:T(8,128)(2,1)S(1)}, f32[16,4096]{1,0:T(8,128)S(...) custom-call(bf16[16,4096]{1,0:T(8,128)(2,1)S(1)} %shard_map.115.refs, ...), custom_call_target="tpu_custom_call" | custom-call | tf_op jit(solution)/shard_map/pallas_call | solution.py:287
  46.4 1.3 %collective-permute-start.30 = (bf16[16,4096]{1,0:T(8,128)(2,1)S(1)}, bf16[16,4096]{1,0:T(8,128)(2,1)S(1)}, u32[]{:S(2)}, u32[]{:S(2)}) collective-permute-start(bf16[16,4096]{1,0:T(8,128)(2,1)S(1)} %get-tuple-element.73), channel_id=1, source_target_pairs={{0,4},{8,0},{16,8},{24,16},{28,24},{20,28},{12,20},{4,12},{1,5},{9... | collective-permute-start | bytes 393224 | tf_op jit(solution)/shard_map/ppermute | solution.py:304
  47.6 0.8 collective-permute-start.34
  48.5 1.6 %collective-permute-start.11 = (bf16[16,4096]{1,0:T(8,128)(2,1)S(1)}, bf16[16,4096]{1,0:T(8,128)(2,1)S(1)}, u32[]{:S(2)}, u32[]{:S(2)}) collective-permute-start(bf16[16,4096]{1,0:T(8,128)(2,1)S(1)} %add_convert_fusion.9), channel_id=1, source_target_pairs={{0,8},{8,16},{16,24},{24,28},{28,20},{20,12},{12,4},{4,0},{1,9},{9... | collective-permute-start | bytes 393224 | tf_op jit(solution)/shard_map/ppermute | solution.py:304
  50.8 2.6 %collective-permute-done.30 = bf16[16,4096]{1,0:T(8,128)(2,1)S(1)} collective-permute-done((bf16[16,4096]{1,0:T(8,128)(2,1)S(1)}, bf16[16,4096]{1,0:T(8,128)(2,1)S(1)}, u32[]{:S(2)}, u32[]{:S(2)}) %collective-permute-start.30) | collective-permute-done | bytes 131104 | tf_op jit(solution)/shard_map/ppermute | solution.py:304
  53.4 0.6 collective-permute-start.31
  54.0 1.5 %collective-permute-start.35 = (bf16[16,4096]{1,0:T(8,128)(2,1)S(1)}, bf16[16,4096]{1,0:T(8,128)(2,1)S(1)}, u32[]{:S(2)}, u32[]{:S(2)}) collective-permute-start(bf16[16,4096]{1,0:T(8,128)(2,1)S(1)} %add_convert_fusion.1), channel_id=1, source_target_pairs={{0,8},{8,16},{16,24},{24,28},{28,20},{20,12},{12,4},{4,0},{1,9},{9... | collective-permute-start | bytes 393224 | tf_op jit(solution)/shard_map/ppermute | solution.py:304
  55.5 1.2 %collective-permute-done.11 = bf16[16,4096]{1,0:T(8,128)(2,1)S(1)} collective-permute-done((bf16[16,4096]{1,0:T(8,128)(2,1)S(1)}, bf16[16,4096]{1,0:T(8,128)(2,1)S(1)}, u32[]{:S(2)}, u32[]{:S(2)}) %collective-permute-start.11) | collective-permute-done | bytes 131104 | tf_op jit(solution)/shard_map/ppermute | solution.py:304
  57.1 1.9 %collective-permute-start.16 = (bf16[16,4096]{1,0:T(8,128)(2,1)S(1)}, bf16[16,4096]{1,0:T(8,128)(2,1)S(1)}, u32[]{:S(2)}, u32[]{:S(2)}) collective-permute-start(bf16[16,4096]{1,0:T(8,128)(2,1)S(1)} %add_convert_fusion.5), channel_id=1, source_target_pairs={{0,4},{8,0},{16,8},{24,16},{28,24},{20,28},{12,20},{4,12},{1,5},{9... | collective-permute-start | bytes 393224 | tf_op jit(solution)/shard_map/ppermute | solution.py:304
  59.2 1.4 %collective-permute-start.32 = (bf16[16,4096]{1,0:T(8,128)(2,1)S(1)}, bf16[16,4096]{1,0:T(8,128)(2,1)S(1)}, u32[]{:S(2)}, u32[]{:S(2)}) collective-permute-start(bf16[16,4096]{1,0:T(8,128)(2,1)S(1)} %add_convert_fusion.3), channel_id=1, source_target_pairs={{0,4},{8,0},{16,8},{24,16},{28,24},{20,28},{12,20},{4,12},{1,5},{9... | collective-permute-start | bytes 393224 | tf_op jit(solution)/shard_map/ppermute | solution.py:304
  60.6 0.7 collective-permute-start.36
  61.3 3.6 %collective-permute-done.32 = bf16[16,4096]{1,0:T(8,128)(2,1)S(1)} collective-permute-done((bf16[16,4096]{1,0:T(8,128)(2,1)S(1)}, bf16[16,4096]{1,0:T(8,128)(2,1)S(1)}, u32[]{:S(2)}, u32[]{:S(2)}) %collective-permute-start.32) | collective-permute-done | bytes 131104 | tf_op jit(solution)/shard_map/ppermute | solution.py:304
  65.0 0.9 %collective-permute-start.33 = (bf16[16,4096]{1,0:T(8,128)(2,1)S(1)}, bf16[16,4096]{1,0:T(8,128)(2,1)S(1)}, u32[]{:S(2)}, u32[]{:S(2)}) collective-permute-start(bf16[16,4096]{1,0:T(8,128)(2,1)S(1)} %add_convert_fusion.2), channel_id=1, source_target_pairs={{0,4},{8,0},{16,8},{24,16},{28,24},{20,28},{12,20},{4,12},{1,5},{9... | collective-permute-start | bytes 393224 | tf_op jit(solution)/shard_map/ppermute | solution.py:304
  65.9 1.2 %collective-permute-start.13 = (bf16[16,4096]{1,0:T(8,128)(2,1)S(1)}, bf16[16,4096]{1,0:T(8,128)(2,1)S(1)}, u32[]{:S(2)}, u32[]{:S(2)}) collective-permute-start(bf16[16,4096]{1,0:T(8,128)(2,1)S(1)} %add_convert_fusion.7), channel_id=1, source_target_pairs={{0,8},{8,16},{16,24},{24,28},{28,20},{20,12},{12,4},{4,0},{1,9},{9... | collective-permute-start | bytes 393224 | tf_op jit(solution)/shard_map/ppermute | solution.py:304
  67.1 2.9 %collective-permute-done.33.ahead_ref = bf16[16,4096]{1,0:T(8,128)(2,1)S(1)} collective-permute-done((bf16[16,4096]{1,0:T(8,128)(2,1)S(1)}, bf16[16,4096]{1,0:T(8,128)(2,1)S(1)}, u32[]{:S(2)}, u32[]{:S(2)}) %collective-permute-start.33) | collective-permute-done | bytes 131104 | tf_op jit(solution)/shard_map/ppermute | solution.py:304
  70.1 1.3 %collective-permute-start.38 = (bf16[4,4096]{1,0:T(4,128)(2,1)S(1)}, bf16[4,4096]{1,0:T(4,128)(2,1)S(1)}, u32[]{:S(2)}, u32[]{:S(2)}) collective-permute-start(bf16[4,4096]{1,0:T(4,128)(2,1)S(1)} %get-tuple-element.82), channel_id=1, source_target_pairs={{0,2},{1,3},{2,0},{3,1},{4,6},{5,7},{6,4},{7,5},{8,10},{9,11},{10,... | collective-permute-start | bytes 98312 | tf_op jit(solution)/shard_map/ppermute | solution.py:351
  72.5 1.3 %collective-permute-start.18 = (bf16[4,4096]{1,0:T(4,128)(2,1)S(1)}, bf16[4,4096]{1,0:T(4,128)(2,1)S(1)}, u32[]{:S(2)}, u32[]{:S(2)}) collective-permute-start(bf16[4,4096]{1,0:T(4,128)(2,1)S(1)} %get-tuple-element.64), channel_id=1, source_target_pairs={{0,2},{1,3},{2,0},{3,1},{4,6},{5,7},{6,4},{7,5},{8,10},{9,11},{10,... | collective-permute-start | bytes 98312 | tf_op jit(solution)/shard_map/ppermute | solution.py:351
  74.0 1.6 %shard_map.123 = bf16[256,4096]{1,0:T(8,128)(2,1)} custom-call(bf16[128,256]{1,0:T(8,128)(2,1)S(1)} %get-tuple-element.89.refs_0_, bf16[128,4096]{1,0:T(8,128)(2,1)S(1)} %get-tuple-element.90.refs_1_), custom_call_target="tpu_custom_call" | custom-call | tf_op jit(solution)/shard_map/pallas_call | solution.py:206
  75.6 2.5 %shard_map.122 = (bf16[4096,256]{1,0:T(8,128)(2,1)}, bf16[4096,256]{1,0:T(8,128)(2,1)}) custom-call(bf16[128,4096]{1,0:T(8,128)(2,1)S(1)} %get-tuple-element.84.refs_0_.refs_2_, bf16[128,256]{1,0:T(8,128)(2,1)S(1)} %get-tuple-element.85.refs_1_, bf16[128,4096]{1,0:T(8,128)(2,1)S(1)} %get-tuple-element.84.refs_0_.refs_2_, ...), custom_call_target="tpu_custom_call" | custom-call | tf_op jit(solution)/shard_map/pallas_call | solution.py:206
  78.1 1.2 %shard_map.121 = bf16[128,4096]{1,0:T(8,128)(2,1)} custom-call(bf16[16,128]{1,0:T(8,128)(2,1)S(1)} %get-tuple-element.48.refs_0_, bf16[4,4096]{1,0:T(4,128)(2,1)S(1)} %get-tuple-element.80.refs_1_, bf16[4,4096]{1,0:T(4,128)(2,1)S(1)} %collective-permute-done.37.refs_2_, bf16[4,4096]{1,0:T(4,128)(2,1)S(1)} %collective-permute-done.38.refs_3_, ...), custom_call_target="tpu_custom_call" | custom-call | tf_op jit(solution)/shard_map/pallas_call | solution.py:177
  79.4 1.3 %shard_map.114 = bf16[128,4096]{1,0:T(8,128)(2,1)} custom-call(bf16[16,128]{1,0:T(8,128)(2,1)S(1)} %get-tuple-element.48.refs_0_, f32[16,128]{1,0:T(8,128)S(1)} %get-tuple-element.49.refs_1_, bf16[4,4096]{1,0:T(4,128)(2,1)S(1)} %get-tuple-element.62.refs_2_, bf16[4,4096]{1,0:T(4,128)(2,1)S(1)} %collective-permute-done.17.refs_3_, ...), custom_call_target="tpu_custom_call" | custom-call | tf_op jit(solution)/shard_map/pallas_call | solution.py:177
  (62 shorter events, 6.9 us)
Async XLA Ops:
  0.6 35.8 %copy-start = (bf16[1,4096,256]{2,1,0:T(8,128)(2,1)S(1)}, bf16[1,4096,256]{2,1,0:T(8,128)(2,1)}, u32[]{:S(2)}) copy-start(bf16[1,4096,256]{2,1,0:T(8,128)(2,1)} %param.10) | copy-start | bytes 6291460
  2.7 3.2 %collective-permute-start = (bf16[4,4096]{1,0:T(4,128)(2,1)S(1)}, bf16[4,4096]{1,0:T(4,128)(2,1)S(1)}, u32[]{:S(2)}, u32[]{:S(2)}) collective-permute-start(bf16[4,4096]{1,0:T(4,128)(2,1)S(1)} %get-tuple-element.51), channel_id=1, source_target_pairs={{0,1},{1,0},{2,3},{3,2},{4,5},{5,4},{6,7},{7,6},{8,9},{9,8},{10,11... | collective-permute-start | bytes 98312 | tf_op jit(solution)/shard_map/ppermute | solution.py:351
  3.2 4.6 %collective-permute-start.1 = (bf16[4,4096]{1,0:T(4,128)(2,1)S(1)}, bf16[4,4096]{1,0:T(4,128)(2,1)S(1)}, u32[]{:S(2)}, u32[]{:S(2)}) collective-permute-start(bf16[4,4096]{1,0:T(4,128)(2,1)S(1)} %get-tuple-element.52), channel_id=1, source_target_pairs={{0,2},{1,3},{2,0},{3,1},{4,6},{5,7},{6,4},{7,5},{8,10},{9,11},{10,... | collective-permute-start | bytes 98312 | tf_op jit(solution)/shard_map/ppermute | solution.py:351
  5.8 3.4 %collective-permute-start.2 = (bf16[4,4096]{1,0:T(4,128)(2,1)S(1)}, bf16[4,4096]{1,0:T(4,128)(2,1)S(1)}, u32[]{:S(2)}, u32[]{:S(2)}) collective-permute-start(bf16[4,4096]{1,0:T(4,128)(2,1)S(1)} %get-tuple-element.53), channel_id=1, source_target_pairs={{0,3},{1,2},{2,1},{3,0},{4,7},{5,6},{6,5},{7,4},{8,11},{9,10},{10,... | collective-permute-start | bytes 98312 | tf_op jit(solution)/shard_map/ppermute | solution.py:351
  9.2 8.0 %collective-permute-start.6 = (bf16[16,4096]{1,0:T(8,128)(2,1)S(1)}, bf16[16,4096]{1,0:T(8,128)(2,1)S(1)}, u32[]{:S(2)}, u32[]{:S(2)}) collective-permute-start(bf16[16,4096]{1,0:T(8,128)(2,1)S(1)} %shard_map.111.refs_0_), channel_id=1, source_target_pairs={{0,8},{8,16},{16,24},{24,28},{28,20},{20,12},{12,4},{4,0},{1,9},{9... | collective-permute-start | bytes 393224 | tf_op jit(solution)/shard_map/ppermute | solution.py:304
  10.8 1.9 %collective-permute-start.20 = (bf16[4,4096]{1,0:T(4,128)(2,1)S(1)}, bf16[4,4096]{1,0:T(4,128)(2,1)S(1)}, u32[]{:S(2)}, u32[]{:S(2)}) collective-permute-start(bf16[4,4096]{1,0:T(4,128)(2,1)S(1)} %get-tuple-element.67), channel_id=1, source_target_pairs={{0,1},{1,0},{2,3},{3,2},{4,5},{5,4},{6,7},{7,6},{8,9},{9,8},{10,11... | collective-permute-start | bytes 98312 | tf_op jit(solution)/shard_map/ppermute | solution.py:351
  10.8 4.0 %collective-permute-start.21 = (bf16[4,4096]{1,0:T(4,128)(2,1)S(1)}, bf16[4,4096]{1,0:T(4,128)(2,1)S(1)}, u32[]{:S(2)}, u32[]{:S(2)}) collective-permute-start(bf16[4,4096]{1,0:T(4,128)(2,1)S(1)} %get-tuple-element.68), channel_id=1, source_target_pairs={{0,2},{1,3},{2,0},{3,1},{4,6},{5,7},{6,4},{7,5},{8,10},{9,11},{10,... | collective-permute-start | bytes 98312 | tf_op jit(solution)/shard_map/ppermute | solution.py:351
  11.7 3.4 %collective-permute-start.22 = (bf16[4,4096]{1,0:T(4,128)(2,1)S(1)}, bf16[4,4096]{1,0:T(4,128)(2,1)S(1)}, u32[]{:S(2)}, u32[]{:S(2)}) collective-permute-start(bf16[4,4096]{1,0:T(4,128)(2,1)S(1)} %get-tuple-element.69), channel_id=1, source_target_pairs={{0,3},{1,2},{2,1},{3,0},{4,7},{5,6},{6,5},{7,4},{8,11},{9,10},{10,... | collective-permute-start | bytes 98312 | tf_op jit(solution)/shard_map/ppermute | solution.py:351
  15.2 6.4 %collective-permute-start.23 = (bf16[16,4096]{1,0:T(8,128)(2,1)S(1)}, bf16[16,4096]{1,0:T(8,128)(2,1)S(1)}, u32[]{:S(2)}, u32[]{:S(2)}) collective-permute-start(bf16[16,4096]{1,0:T(8,128)(2,1)S(1)} %shard_map.115.refs_0_), channel_id=1, source_target_pairs={{0,4},{8,0},{16,8},{24,16},{28,24},{20,28},{12,20},{4,12},{1,5},{9... | collective-permute-start | bytes 393224 | tf_op jit(solution)/shard_map/ppermute | solution.py:304
  15.8 8.6 %collective-permute-start.3 = (bf16[16,4096]{1,0:T(8,128)(2,1)S(1)}, bf16[16,4096]{1,0:T(8,128)(2,1)S(1)}, u32[]{:S(2)}, u32[]{:S(2)}) collective-permute-start(bf16[16,4096]{1,0:T(8,128)(2,1)S(1)} %shard_map.111.refs_0_), channel_id=1, source_target_pairs={{0,4},{8,0},{16,8},{24,16},{28,24},{20,28},{12,20},{4,12},{1,5},{9... | collective-permute-start | bytes 393224 | tf_op jit(solution)/shard_map/ppermute | solution.py:304
  17.2 7.8 %collective-permute-start.7 = (bf16[16,4096]{1,0:T(8,128)(2,1)S(1)}, bf16[16,4096]{1,0:T(8,128)(2,1)S(1)}, u32[]{:S(2)}, u32[]{:S(2)}) collective-permute-start(bf16[16,4096]{1,0:T(8,128)(2,1)S(1)} %collective-permute-done.6.refs_7_), channel_id=1, source_target_pairs={{0,8},{8,16},{16,24},{24,28},{28,20},{20,12},{12,4},{4,0},{1,9},{9... | collective-permute-start | bytes 393224 | tf_op jit(solution)/shard_map/ppermute | solution.py:304
  17.8 8.6 %collective-permute-start.27 = (bf16[16,4096]{1,0:T(8,128)(2,1)S(1)}, bf16[16,4096]{1,0:T(8,128)(2,1)S(1)}, u32[]{:S(2)}, u32[]{:S(2)}) collective-permute-start(bf16[16,4096]{1,0:T(8,128)(2,1)S(1)} %shard_map.115.refs_0_), channel_id=1, source_target_pairs={{0,8},{8,16},{16,24},{24,28},{28,20},{20,12},{12,4},{4,0},{1,9},{9... | collective-permute-start | bytes 393224 | tf_op jit(solution)/shard_map/ppermute | solution.py:304
  21.6 6.4 %collective-permute-start.24 = (bf16[16,4096]{1,0:T(8,128)(2,1)S(1)}, bf16[16,4096]{1,0:T(8,128)(2,1)S(1)}, u32[]{:S(2)}, u32[]{:S(2)}) collective-permute-start(bf16[16,4096]{1,0:T(8,128)(2,1)S(1)} %collective-permute-done.23.refs_1_), channel_id=1, source_target_pairs={{0,4},{8,0},{16,8},{24,16},{28,24},{20,28},{12,20},{4,12},{1,5},{9... | collective-permute-start | bytes 393224 | tf_op jit(solution)/shard_map/ppermute | solution.py:304
  24.4 6.1 %collective-permute-start.4 = (bf16[16,4096]{1,0:T(8,128)(2,1)S(1)}, bf16[16,4096]{1,0:T(8,128)(2,1)S(1)}, u32[]{:S(2)}, u32[]{:S(2)}) collective-permute-start(bf16[16,4096]{1,0:T(8,128)(2,1)S(1)} %collective-permute-done.3.refs_1_), channel_id=1, source_target_pairs={{0,4},{8,0},{16,8},{24,16},{28,24},{20,28},{12,20},{4,12},{1,5},{9... | collective-permute-start | bytes 393224 | tf_op jit(solution)/shard_map/ppermute | solution.py:304
  25.0 6.2 %collective-permute-start.8 = (bf16[16,4096]{1,0:T(8,128)(2,1)S(1)}, bf16[16,4096]{1,0:T(8,128)(2,1)S(1)}, u32[]{:S(2)}, u32[]{:S(2)}) collective-permute-start(bf16[16,4096]{1,0:T(8,128)(2,1)S(1)} %collective-permute-done.7.refs_6_), channel_id=1, source_target_pairs={{0,8},{8,16},{16,24},{24,28},{28,20},{20,12},{12,4},{4,0},{1,9},{9... | collective-permute-start | bytes 393224 | tf_op jit(solution)/shard_map/ppermute | solution.py:304
  26.4 6.1 %collective-permute-start.28 = (bf16[16,4096]{1,0:T(8,128)(2,1)S(1)}, bf16[16,4096]{1,0:T(8,128)(2,1)S(1)}, u32[]{:S(2)}, u32[]{:S(2)}) collective-permute-start(bf16[16,4096]{1,0:T(8,128)(2,1)S(1)} %collective-permute-done.27.refs_7_), channel_id=1, source_target_pairs={{0,8},{8,16},{16,24},{24,28},{28,20},{20,12},{12,4},{4,0},{1,9},{9... | collective-permute-start | bytes 393224 | tf_op jit(solution)/shard_map/ppermute | solution.py:304
  28.0 6.1 %collective-permute-start.25 = (bf16[16,4096]{1,0:T(8,128)(2,1)S(1)}, bf16[16,4096]{1,0:T(8,128)(2,1)S(1)}, u32[]{:S(2)}, u32[]{:S(2)}) collective-permute-start(bf16[16,4096]{1,0:T(8,128)(2,1)S(1)} %collective-permute-done.24.refs_2_), channel_id=1, source_target_pairs={{0,4},{8,0},{16,8},{24,16},{28,24},{20,28},{12,20},{4,12},{1,5},{9... | collective-permute-start | bytes 393224 | tf_op jit(solution)/shard_map/ppermute | solution.py:304
  30.5 5.9 %collective-permute-start.5 = (bf16[16,4096]{1,0:T(8,128)(2,1)S(1)}, bf16[16,4096]{1,0:T(8,128)(2,1)S(1)}, u32[]{:S(2)}, u32[]{:S(2)}) collective-permute-start(bf16[16,4096]{1,0:T(8,128)(2,1)S(1)} %collective-permute-done.4.refs_2_), channel_id=1, source_target_pairs={{0,4},{8,0},{16,8},{24,16},{28,24},{20,28},{12,20},{4,12},{1,5},{9... | collective-permute-start | bytes 393224 | tf_op jit(solution)/shard_map/ppermute | solution.py:304
  31.2 5.2 %collective-permute-start.9 = (bf16[16,4096]{1,0:T(8,128)(2,1)S(1)}, bf16[16,4096]{1,0:T(8,128)(2,1)S(1)}, u32[]{:S(2)}, u32[]{:S(2)}) collective-permute-start(bf16[16,4096]{1,0:T(8,128)(2,1)S(1)} %collective-permute-done.8.refs_5_), channel_id=1, source_target_pairs={{0,8},{8,16},{16,24},{24,28},{28,20},{20,12},{12,4},{4,0},{1,9},{9... | collective-permute-start | bytes 393224 | tf_op jit(solution)/shard_map/ppermute | solution.py:304
  32.5 12.2 %collective-permute-start.29 = (bf16[16,4096]{1,0:T(8,128)(2,1)S(1)}, bf16[16,4096]{1,0:T(8,128)(2,1)S(1)}, u32[]{:S(2)}, u32[]{:S(2)}) collective-permute-start(bf16[16,4096]{1,0:T(8,128)(2,1)S(1)} %collective-permute-done.28.refs_6_), channel_id=1, source_target_pairs={{0,8},{8,16},{16,24},{24,28},{28,20},{20,12},{12,4},{4,0},{1,9},{9... | collective-permute-start | bytes 393224 | tf_op jit(solution)/shard_map/ppermute | solution.py:304
  34.1 10.6 %collective-permute-start.26 = (bf16[16,4096]{1,0:T(8,128)(2,1)S(1)}, bf16[16,4096]{1,0:T(8,128)(2,1)S(1)}, u32[]{:S(2)}, u32[]{:S(2)}) collective-permute-start(bf16[16,4096]{1,0:T(8,128)(2,1)S(1)} %collective-permute-done.25.refs_3_), channel_id=1, source_target_pairs={{0,4},{8,0},{16,8},{24,16},{28,24},{20,28},{12,20},{4,12},{1,5},{9... | collective-permute-start | bytes 393224 | tf_op jit(solution)/shard_map/ppermute | solution.py:304
  36.4 1.6 %copy-start.1 = (bf16[1,4096,256]{2,1,0:T(8,128)(2,1)S(1)}, bf16[1,4096,256]{2,1,0:T(8,128)(2,1)}, u32[]{:S(2)}) copy-start(bf16[1,4096,256]{2,1,0:T(8,128)(2,1)} %param.11) | copy-start | bytes 6291460
  38.0 1.6 %copy-start.2 = (bf16[1,256,4096]{2,1,0:T(8,128)(2,1)S(1)}, bf16[1,256,4096]{2,1,0:T(8,128)(2,1)}, u32[]{:S(2)}) copy-start(bf16[1,256,4096]{2,1,0:T(8,128)(2,1)} %param.12) | copy-start | bytes 6291460
  40.7 7.7 %collective-permute-start.10 = (bf16[16,4096]{1,0:T(8,128)(2,1)S(1)}, bf16[16,4096]{1,0:T(8,128)(2,1)S(1)}, u32[]{:S(2)}, u32[]{:S(2)}) collective-permute-start(bf16[16,4096]{1,0:T(8,128)(2,1)S(1)} %get-tuple-element.55), channel_id=1, source_target_pairs={{0,8},{8,16},{16,24},{24,28},{28,20},{20,12},{12,4},{4,0},{1,9},{9... | collective-permute-start | bytes 393224 | tf_op jit(solution)/shard_map/ppermute | solution.py:304
  44.2 6.3 %collective-permute-start.14 = (bf16[16,4096]{1,0:T(8,128)(2,1)S(1)}, bf16[16,4096]{1,0:T(8,128)(2,1)S(1)}, u32[]{:S(2)}, u32[]{:S(2)}) collective-permute-start(bf16[16,4096]{1,0:T(8,128)(2,1)S(1)} %get-tuple-element.59), channel_id=1, source_target_pairs={{0,4},{8,0},{16,8},{24,16},{28,24},{20,28},{12,20},{4,12},{1,5},{9... | collective-permute-start | bytes 393224 | tf_op jit(solution)/shard_map/ppermute | solution.py:304
  46.4 7.0 %collective-permute-start.30 = (bf16[16,4096]{1,0:T(8,128)(2,1)S(1)}, bf16[16,4096]{1,0:T(8,128)(2,1)S(1)}, u32[]{:S(2)}, u32[]{:S(2)}) collective-permute-start(bf16[16,4096]{1,0:T(8,128)(2,1)S(1)} %get-tuple-element.73), channel_id=1, source_target_pairs={{0,4},{8,0},{16,8},{24,16},{28,24},{20,28},{12,20},{4,12},{1,5},{9... | collective-permute-start | bytes 393224 | tf_op jit(solution)/shard_map/ppermute | solution.py:304
  47.6 6.4 %collective-permute-start.34 = (bf16[16,4096]{1,0:T(8,128)(2,1)S(1)}, bf16[16,4096]{1,0:T(8,128)(2,1)S(1)}, u32[]{:S(2)}, u32[]{:S(2)}) collective-permute-start(bf16[16,4096]{1,0:T(8,128)(2,1)S(1)} %get-tuple-element.77), channel_id=1, source_target_pairs={{0,8},{8,16},{16,24},{24,28},{28,20},{20,12},{12,4},{4,0},{1,9},{9... | collective-permute-start | bytes 393224 | tf_op jit(solution)/shard_map/ppermute | solution.py:304
  48.5 8.3 %collective-permute-start.11 = (bf16[16,4096]{1,0:T(8,128)(2,1)S(1)}, bf16[16,4096]{1,0:T(8,128)(2,1)S(1)}, u32[]{:S(2)}, u32[]{:S(2)}) collective-permute-start(bf16[16,4096]{1,0:T(8,128)(2,1)S(1)} %add_convert_fusion.9), channel_id=1, source_target_pairs={{0,8},{8,16},{16,24},{24,28},{28,20},{20,12},{12,4},{4,0},{1,9},{9... | collective-permute-start | bytes 393224 | tf_op jit(solution)/shard_map/ppermute | solution.py:304
  50.6 6.5 %collective-permute-start.15 = (bf16[16,4096]{1,0:T(8,128)(2,1)S(1)}, bf16[16,4096]{1,0:T(8,128)(2,1)S(1)}, u32[]{:S(2)}, u32[]{:S(2)}) collective-permute-start(bf16[16,4096]{1,0:T(8,128)(2,1)S(1)} %add_convert_fusion.6), channel_id=1, source_target_pairs={{0,4},{8,0},{16,8},{24,16},{28,24},{20,28},{12,20},{4,12},{1,5},{9... | collective-permute-start | bytes 393224 | tf_op jit(solution)/shard_map/ppermute | solution.py:304
  53.4 5.8 %collective-permute-start.31 = (bf16[16,4096]{1,0:T(8,128)(2,1)S(1)}, bf16[16,4096]{1,0:T(8,128)(2,1)S(1)}, u32[]{:S(2)}, u32[]{:S(2)}) collective-permute-start(bf16[16,4096]{1,0:T(8,128)(2,1)S(1)} %add_convert_fusion.4), channel_id=1, source_target_pairs={{0,4},{8,0},{16,8},{24,16},{28,24},{20,28},{12,20},{4,12},{1,5},{9... | collective-permute-start | bytes 393224 | tf_op jit(solution)/shard_map/ppermute | solution.py:304
  54.0 6.5 %collective-permute-start.35 = (bf16[16,4096]{1,0:T(8,128)(2,1)S(1)}, bf16[16,4096]{1,0:T(8,128)(2,1)S(1)}, u32[]{:S(2)}, u32[]{:S(2)}) collective-permute-start(bf16[16,4096]{1,0:T(8,128)(2,1)S(1)} %add_convert_fusion.1), channel_id=1, source_target_pairs={{0,8},{8,16},{16,24},{24,28},{28,20},{20,12},{12,4},{4,0},{1,9},{9... | collective-permute-start | bytes 393224 | tf_op jit(solution)/shard_map/ppermute | solution.py:304
  56.8 9.0 %collective-permute-start.12 = (bf16[16,4096]{1,0:T(8,128)(2,1)S(1)}, bf16[16,4096]{1,0:T(8,128)(2,1)S(1)}, u32[]{:S(2)}, u32[]{:S(2)}) collective-permute-start(bf16[16,4096]{1,0:T(8,128)(2,1)S(1)} %add_convert_fusion.8), channel_id=1, source_target_pairs={{0,8},{8,16},{16,24},{24,28},{28,20},{20,12},{12,4},{4,0},{1,9},{9... | collective-permute-start | bytes 393224 | tf_op jit(solution)/shard_map/ppermute | solution.py:304
  57.1 14.9 %collective-permute-start.16 = (bf16[16,4096]{1,0:T(8,128)(2,1)S(1)}, bf16[16,4096]{1,0:T(8,128)(2,1)S(1)}, u32[]{:S(2)}, u32[]{:S(2)}) collective-permute-start(bf16[16,4096]{1,0:T(8,128)(2,1)S(1)} %add_convert_fusion.5), channel_id=1, source_target_pairs={{0,4},{8,0},{16,8},{24,16},{28,24},{20,28},{12,20},{4,12},{1,5},{9... | collective-permute-start | bytes 393224 | tf_op jit(solution)/shard_map/ppermute | solution.py:304
  59.2 5.8 %collective-permute-start.32 = (bf16[16,4096]{1,0:T(8,128)(2,1)S(1)}, bf16[16,4096]{1,0:T(8,128)(2,1)S(1)}, u32[]{:S(2)}, u32[]{:S(2)}) collective-permute-start(bf16[16,4096]{1,0:T(8,128)(2,1)S(1)} %add_convert_fusion.3), channel_id=1, source_target_pairs={{0,4},{8,0},{16,8},{24,16},{28,24},{20,28},{12,20},{4,12},{1,5},{9... | collective-permute-start | bytes 393224 | tf_op jit(solution)/shard_map/ppermute | solution.py:304
  60.6 6.5 %collective-permute-start.36 = (bf16[16,4096]{1,0:T(8,128)(2,1)S(1)}, bf16[16,4096]{1,0:T(8,128)(2,1)S(1)}, u32[]{:S(2)}, u32[]{:S(2)}) collective-permute-start(bf16[16,4096]{1,0:T(8,128)(2,1)S(1)} %add_convert_fusion), channel_id=1, source_target_pairs={{0,8},{8,16},{16,24},{24,28},{28,20},{20,12},{12,4},{4,0},{1,9},{9... | collective-permute-start | bytes 393224 | tf_op jit(solution)/shard_map/ppermute | solution.py:304
  65.0 5.0 %collective-permute-start.33 = (bf16[16,4096]{1,0:T(8,128)(2,1)S(1)}, bf16[16,4096]{1,0:T(8,128)(2,1)S(1)}, u32[]{:S(2)}, u32[]{:S(2)}) collective-permute-start(bf16[16,4096]{1,0:T(8,128)(2,1)S(1)} %add_convert_fusion.2), channel_id=1, source_target_pairs={{0,4},{8,0},{16,8},{24,16},{28,24},{20,28},{12,20},{4,12},{1,5},{9... | collective-permute-start | bytes 393224 | tf_op jit(solution)/shard_map/ppermute | solution.py:304
  65.9 6.1 %collective-permute-start.13 = (bf16[16,4096]{1,0:T(8,128)(2,1)S(1)}, bf16[16,4096]{1,0:T(8,128)(2,1)S(1)}, u32[]{:S(2)}, u32[]{:S(2)}) collective-permute-start(bf16[16,4096]{1,0:T(8,128)(2,1)S(1)} %add_convert_fusion.7), channel_id=1, source_target_pairs={{0,8},{8,16},{16,24},{24,28},{28,20},{20,12},{12,4},{4,0},{1,9},{9... | collective-permute-start | bytes 393224 | tf_op jit(solution)/shard_map/ppermute | solution.py:304
  70.0 3.7 %collective-permute-start.37 = (bf16[4,4096]{1,0:T(4,128)(2,1)S(1)}, bf16[4,4096]{1,0:T(4,128)(2,1)S(1)}, u32[]{:S(2)}, u32[]{:S(2)}) collective-permute-start(bf16[4,4096]{1,0:T(4,128)(2,1)S(1)} %get-tuple-element.81), channel_id=1, source_target_pairs={{0,1},{1,0},{2,3},{3,2},{4,5},{5,4},{6,7},{7,6},{8,9},{9,8},{10,11... | collective-permute-start | bytes 98312 | tf_op jit(solution)/shard_map/ppermute | solution.py:351
  70.1 7.9 %collective-permute-start.38 = (bf16[4,4096]{1,0:T(4,128)(2,1)S(1)}, bf16[4,4096]{1,0:T(4,128)(2,1)S(1)}, u32[]{:S(2)}, u32[]{:S(2)}) collective-permute-start(bf16[4,4096]{1,0:T(4,128)(2,1)S(1)} %get-tuple-element.82), channel_id=1, source_target_pairs={{0,2},{1,3},{2,0},{3,1},{4,6},{5,7},{6,4},{7,5},{8,10},{9,11},{10,... | collective-permute-start | bytes 98312 | tf_op jit(solution)/shard_map/ppermute | solution.py:351
  71.4 6.6 %collective-permute-start.39 = (bf16[4,4096]{1,0:T(4,128)(2,1)S(1)}, bf16[4,4096]{1,0:T(4,128)(2,1)S(1)}, u32[]{:S(2)}, u32[]{:S(2)}) collective-permute-start(bf16[4,4096]{1,0:T(4,128)(2,1)S(1)} %get-tuple-element.83), channel_id=1, source_target_pairs={{0,3},{1,2},{2,1},{3,0},{4,7},{5,6},{6,5},{7,4},{8,11},{9,10},{10,... | collective-permute-start | bytes 98312 | tf_op jit(solution)/shard_map/ppermute | solution.py:351
  72.0 7.3 %collective-permute-start.17 = (bf16[4,4096]{1,0:T(4,128)(2,1)S(1)}, bf16[4,4096]{1,0:T(4,128)(2,1)S(1)}, u32[]{:S(2)}, u32[]{:S(2)}) collective-permute-start(bf16[4,4096]{1,0:T(4,128)(2,1)S(1)} %get-tuple-element.63), channel_id=1, source_target_pairs={{0,1},{1,0},{2,3},{3,2},{4,5},{5,4},{6,7},{7,6},{8,9},{9,8},{10,11... | collective-permute-start | bytes 98312 | tf_op jit(solution)/shard_map/ppermute | solution.py:351
  72.5 6.9 %collective-permute-start.18 = (bf16[4,4096]{1,0:T(4,128)(2,1)S(1)}, bf16[4,4096]{1,0:T(4,128)(2,1)S(1)}, u32[]{:S(2)}, u32[]{:S(2)}) collective-permute-start(bf16[4,4096]{1,0:T(4,128)(2,1)S(1)} %get-tuple-element.64), channel_id=1, source_target_pairs={{0,2},{1,3},{2,0},{3,1},{4,6},{5,7},{6,4},{7,5},{8,10},{9,11},{10,... | collective-permute-start | bytes 98312 | tf_op jit(solution)/shard_map/ppermute | solution.py:351
  73.7 5.7 %collective-permute-start.19 = (bf16[4,4096]{1,0:T(4,128)(2,1)S(1)}, bf16[4,4096]{1,0:T(4,128)(2,1)S(1)}, u32[]{:S(2)}, u32[]{:S(2)}) collective-permute-start(bf16[4,4096]{1,0:T(4,128)(2,1)S(1)} %get-tuple-element.65), channel_id=1, source_target_pairs={{0,3},{1,2},{2,1},{3,0},{4,7},{5,6},{6,5},{7,4},{8,11},{9,10},{10,... | collective-permute-start | bytes 98312 | tf_op jit(solution)/shard_map/ppermute | solution.py:351
